TPU v7x, 256 devices: a whole 4x4x8 slice. The times are simulated.
256 devices in a mesh: ep: 64 (over z, y, core), tp: 4 (over x).
Axes of the slice: x: 4, y: 4, z: 8, core: 2. Of those that a mesh axis runs over, the one named last changes fastest.
Arguments:
- tokens: bfloat16 [8192, 4096], P('ep', 'tp'), may hold values from -6 to 6
- out_grad: bfloat16 [8192, 4096], P('ep', 'tp'), may hold values from -6 to 6
- expert_ids: int32 [8192, 8], P('ep'), may hold values from 0 to 63, all different within a row; in each aligned block of 128 rows (0 to 127, 128 to 255, ...) at most 18 rows name the same one
- route_probs: float32 [8192, 8], P('ep'), may hold values from 0.05 to 0.5
- w_gate: bfloat16 [64, 4096, 768], P('ep', 'tp'), may hold values from -0.09375 to 0.09375
- w_up: bfloat16 [64, 4096, 768], P('ep', 'tp'), may hold values from -0.09375 to 0.09375
- w_down: bfloat16 [64, 768, 4096], P('ep', None, 'tp'), may hold values from -0.21875 to 0.21875
Outputs:
- grad_tokens: bfloat16 [8192, 4096], P('ep', 'tp')
- fisher_gate: bfloat16 [64, 4096, 768], P('ep', 'tp')
- fisher_up: bfloat16 [64, 4096, 768], P('ep', 'tp')
- fisher_down: bfloat16 [64, 768, 4096], P('ep', None, 'tp')
Inputs may be any that keep to these rules, and one draw needn't show every extreme that they name: `expert_ids`: each token names 8 different experts; among the tokens of one index of ep no expert is named by more than 18 tokens, a bound that some block reaches.
All inputs are finite; a program needn't handle non-finite values.
Results may differ from a plain program's by a relative error of at most 0.03.
Values may be sent and summed in bfloat16 or wider, within the bound.
No kernel may reach another device: no remote copies, remote signals or barrier semaphores. Data moves between devices by JAX's collectives and lax.ppermute only.
A program may use at most 128 MiB of HBM per device.

v0:
```python
import jax
import jax.numpy as jnp
from jax import lax
from jax.sharding import PartitionSpec as P


def contract_rows(left, right):
    return lax.dot_general(
        left, right, (((0,), (0,)), ((), ())), preferred_element_type=jnp.float32
    )


def contract_cols(left, right):
    return lax.dot_general(
        left, right, (((1,), (1,)), ((), ())), preferred_element_type=jnp.float32
    )


def swiglu_back(gate, up, dact):
    sig = jax.nn.sigmoid(gate)
    act = (gate * sig * up).astype(jnp.bfloat16)
    dgate = (dact * up * sig * (1.0 + gate * (1.0 - sig))).astype(jnp.bfloat16)
    dup = (dact * gate * sig).astype(jnp.bfloat16)
    return (act, dgate, dup)


def squared(values):
    return jnp.square(values.astype(jnp.float32)).astype(jnp.bfloat16)


def on_device(tokens, out_grad, expert_ids, route_probs, w_gate, w_up, w_down):
    tok_rows = tokens.shape[0]
    width_part = tokens.shape[1]
    top_count = expert_ids.shape[1]
    experts = lax.axis_size("ep")
    capacity = tok_rows * top_count * 9 // (8 * experts)
    assigns = tok_rows * top_count
    flat_ids = expert_ids.reshape(-1)
    onehot = (flat_ids[:, None] == jnp.arange(experts, dtype=jnp.int32)[None, :]).astype(jnp.int32)
    ranks = jnp.sum((jnp.cumsum(onehot, 0) - onehot) * onehot, 1)
    slot_index = flat_ids * capacity + ranks
    table = (
        jnp.full((experts * capacity,), assigns, jnp.int32)
        .at[slot_index]
        .set(jnp.arange(assigns, dtype=jnp.int32))
    )
    token_of = table // top_count
    padded_x = jnp.concatenate([tokens, jnp.zeros((1, width_part), tokens.dtype)], 0)
    padded_dy = jnp.concatenate([out_grad, jnp.zeros((1, width_part), out_grad.dtype)], 0)
    padded_p = jnp.concatenate([route_probs.reshape(-1), jnp.zeros((1,), jnp.float32)], 0)
    send_x = padded_x[token_of].reshape(experts, capacity, width_part)
    send_dy = (padded_dy[token_of].astype(jnp.float32) * padded_p[table][:, None]).astype(
        jnp.bfloat16
    )
    send_dy = send_dy.reshape(experts, capacity, width_part)
    gate_mat = w_gate[0]
    up_mat = w_up[0]
    down_mat = w_down[0]
    recv_x, recv_dy = (
        lax.all_to_all(send_x, "ep", split_axis=0, concat_axis=0, tiled=True),
        lax.all_to_all(send_dy, "ep", split_axis=0, concat_axis=0, tiled=True),
    )
    recv_x = recv_x.reshape(-1, width_part)
    recv_dy = recv_dy.reshape(-1, width_part)
    gate_part = jnp.dot(recv_x, gate_mat, preferred_element_type=jnp.float32)
    up_part = jnp.dot(recv_x, up_mat, preferred_element_type=jnp.float32)
    dact_part = contract_cols(recv_dy, down_mat)
    gate, up, dact = (
        lax.psum(gate_part.astype(jnp.bfloat16), "tp").astype(jnp.float32),
        lax.psum(up_part.astype(jnp.bfloat16), "tp").astype(jnp.float32),
        lax.psum(dact_part.astype(jnp.bfloat16), "tp").astype(jnp.float32),
    )
    act, dgate, dup = swiglu_back(gate, up, dact)
    dx_rows = (contract_cols(dgate, gate_mat) + contract_cols(dup, up_mat)).astype(jnp.bfloat16)
    returned = lax.all_to_all(
        dx_rows.reshape(experts, capacity, width_part),
        "ep",
        split_axis=0,
        concat_axis=0,
        tiled=True,
    )
    scale = 1.0 / tok_rows
    x_sq = squared(recv_x)
    fisher_gate = (contract_rows(x_sq, squared(dgate)) * scale).astype(jnp.bfloat16)[None]
    fisher_up = (contract_rows(x_sq, squared(dup)) * scale).astype(jnp.bfloat16)[None]
    fisher_down = (contract_rows(squared(act), squared(recv_dy)) * scale).astype(jnp.bfloat16)[None]
    pulled = returned.reshape(experts * capacity, width_part)[slot_index].astype(jnp.float32)
    grad_tokens = jnp.sum(pulled.reshape(tok_rows, top_count, width_part), 1).astype(jnp.bfloat16)
    return (grad_tokens, fisher_gate, fisher_up, fisher_down)


def solution(mesh):
    in_specs = (
        P("ep", "tp"),
        P("ep", "tp"),
        P("ep", None),
        P("ep", None),
        P("ep", "tp", None),
        P("ep", "tp", None),
        P("ep", None, "tp"),
    )
    out_specs = (P("ep", "tp"), P("ep", "tp", None), P("ep", "tp", None), P("ep", None, "tp"))
    return jax.shard_map(
        on_device, mesh=mesh, in_specs=in_specs, out_specs=out_specs, check_vma=False
    )
```

profile of v0, /device:TPU:64, one launch (start us, length us, event | category | flops | bytes accessed | tf_op | source)
XLA Modules:
  0.0 449.5 jit_solution(8603457234124716283)
XLA Ops:
  9.2 18.0 %reduce-window.6 = s32[64,8,128]{2,1,0:T(8,128)S(1)} reduce-window(s32[64,8,128]{2,1,0:T(8,128)S(1)} %fusion.26, s32[]{:T(128)} %constant.17.clone.1), window={size=1x1x128 pad=0_0x0_0x127_0}, to_apply=%region_0.0 | reduce-window | flops 8323072 | bytes 524292 | tf_op jit(solution)/shard_map/reduce-window
  27.9 4.3 scatter_custom_fusion
  32.3 5.0 %gather_fusion.2 = bf16[1152,1024]{1,0:T(8,128)(2,1)} fusion(bf16[129,1024]{1,0:T(8,128)(2,1)S(1)} %concatenate.11, s32[2048]{0:T(1024)S(1)} %get-tuple-element.10), kind=kCustom, calls=%fused_computation.2 | custom fusion | bytes 4723200 | tf_op jit(solution)/shard_map/gather | solution.py:51
  37.3 4.3 reshape.87
  41.5 11.6 %all-to-all-start.1 = ((bf16[64,18,1024]{2,1,0:T(8,128)(2,1)}), bf16[64,18,1024]{2,1,0:T(8,128)(2,1)}, u32[]{:S(2)}, u32[]{:S(2)}) async-start(bf16[64,18,1024]{2,1,0:T(8,128)(2,1)} %reshape.87), calls=%async_computation.1 | async-start | bytes 6291456 | tf_op jit(solution)/shard_map/all_to_all | solution.py:60
  53.4 6.5 %gather_fusion.1 = f32[1152]{0:T(1024)S(1)} fusion(f32[1025]{0:T(1024)S(1)} %pad_maximum_fusion, s32[2048]{0:T(1024)S(1)} %get-tuple-element.9), kind=kCustom, calls=%fused_computation.1 | custom fusion | bytes 13824 | tf_op jit(solution)/shard_map/gather | solution.py:52
  60.0 5.0 %gather_fusion = bf16[1152,1024]{1,0:T(8,128)(2,1)} fusion(bf16[129,1024]{1,0:T(8,128)(2,1)S(1)} %concatenate.9, s32[2048]{0:T(1024)S(1)} %get-tuple-element.10), kind=kCustom, calls=%fused_computation | custom fusion | bytes 4723200 | tf_op jit(solution)/shard_map/gather | solution.py:52
  65.1 4.9 %reshape.91 = f32[64,18,1024]{2,1,0:T(8,128)} reshape(bf16[1152,1024]{1,0:T(8,128)(2,1)} %gather_fusion) | data formatting | bytes 7077888 | tf_op jit(solution)/shard_map/convert_element_type | solution.py:52
  69.9 4.8 %multiply_convert_fusion = bf16[64,18,1024]{2,1,0:T(8,128)(2,1)} fusion(f32[64,18,1024]{2,1,0:T(8,128)} %reshape.91, f32[64,18]{1,0:T(8,128)S(1)} %mul.70), kind=kLoop, calls=%fused_computation.5 | loop fusion | flops 2359296 | bytes 7082496 | tf_op jit(solution)/shard_map/convert_element_type | solution.py:52
  74.8 49.8 %all-to-all-done.1 = bf16[64,18,1024]{2,1,0:T(8,128)(2,1)} async-done(((bf16[64,18,1024]{2,1,0:T(8,128)(2,1)}), bf16[64,18,1024]{2,1,0:T(8,128)(2,1)}, u32[]{:S(2)}, u32[]{:S(2)}) %all-to-all-start.1) | async-done | bytes 2359328 | tf_op jit(solution)/shard_map/all_to_all | solution.py:60
  124.6 7.9 %all-to-all-start = ((bf16[64,18,1024]{2,1,0:T(8,128)(2,1)}), bf16[64,18,1024]{2,1,0:T(8,128)(2,1)}, u32[]{:S(2)}, u32[]{:S(2)}) async-start(bf16[64,18,1024]{2,1,0:T(8,128)(2,1)} %multiply_convert_fusion), calls=%async_computation | async-start | bytes 6291456 | tf_op jit(solution)/shard_map/all_to_all | solution.py:61
  132.7 4.4 reshape.88
  137.1 5.0 %convolution_convert_fusion = bf16[1152,768]{1,0:T(8,128)(2,1)} fusion(bf16[1152,1024]{1,0:T(8,128)(2,1)} %reshape.88, bf16[1,1024,768]{2,1,0:T(8,128)(2,1)S(1)} %copy-done), kind=kOutput, calls=%fused_computation.28 | convolution fusion | flops 1812824064 | bytes 5701632 | tf_op jit(solution)/shard_map/dot_general | solution.py:65
  145.3 58.6 %all-to-all-done = bf16[64,18,1024]{2,1,0:T(8,128)(2,1)} async-done(((bf16[64,18,1024]{2,1,0:T(8,128)(2,1)}), bf16[64,18,1024]{2,1,0:T(8,128)(2,1)}, u32[]{:S(2)}, u32[]{:S(2)}) %all-to-all-start) | async-done | bytes 2359328 | tf_op jit(solution)/shard_map/all_to_all | solution.py:61
  203.9 4.4 reshape.86
  208.3 5.0 %convolution_convert_fusion.2 = bf16[1152,768]{1,0:T(8,128)(2,1)} fusion(bf16[1152,1024]{1,0:T(8,128)(2,1)} %reshape.86, bf16[1,768,1024]{2,1,0:T(8,128)(2,1)S(1)} %copy-done.13), kind=kOutput, calls=%fused_computation.30 | convolution fusion | flops 1812824064 | bytes 5701632 | tf_op jit(solution)/shard_map/dot_general | solution.py:14
  213.4 115.1 %all-reduce.5.cloned.1.call-done = (bf16[1152,768]{1,0:T(8,128)(2,1)}, bf16[1152,768]{1,0:T(8,128)(2,1)}, bf16[1152,768]{1,0:T(8,128)(2,1)}) async-done(((bf16[1152,768]{1,0:T(8,128)(2,1)}, bf16[1152,768]{1,0:T(8,128)(2,1)}, bf16[1152,768]{1,0:T(8,128)(2,1)}), (bf16[1152,768]{1,0:T(8,128)(2,1)}, bf16[1152,768]{1,0:T(8,128)(2,1)}, bf16[1152,768]{1,0:T(8,128)(2,1)})) %all-reduce.5.cloned.1.call-update) | async-done | bytes 5308432 | tf_op jit(solution)/shard_map/psum | solution.py:70
  328.5 4.1 fusion.2
  340.1 4.3 reshape.89
  344.4 10.6 %all-to-all-start.2 = ((bf16[64,18,1024]{2,1,0:T(8,128)(2,1)}), bf16[64,18,1024]{2,1,0:T(8,128)(2,1)}, u32[]{:S(2)}, u32[]{:S(2)}) async-start(bf16[64,18,1024]{2,1,0:T(8,128)(2,1)} %reshape.89), calls=%async_computation.2 | async-start | bytes 6291456 | tf_op jit(solution)/shard_map/all_to_all | solution.py:75
  355.0 5.8 %fusion.20 = bf16[1,1024,768]{2,1,0:T(8,128)(2,1)} fusion(bf16[1152,768]{1,0:T(8,128)(2,1)} %copy-done.9, bf16[1152,1024]{1,0:T(8,128)(2,1)} %reshape.88), kind=kOutput, calls=%fused_computation.44 | convolution fusion | flops 1819705344 | bytes 5701632 | tf_op jit(solution)/shard_map/dot_general | solution.py:8
  368.4 58.0 %all-to-all-done.2 = bf16[64,18,1024]{2,1,0:T(8,128)(2,1)} async-done(((bf16[64,18,1024]{2,1,0:T(8,128)(2,1)}), bf16[64,18,1024]{2,1,0:T(8,128)(2,1)}, u32[]{:S(2)}, u32[]{:S(2)}) %all-to-all-start.2) | async-done | bytes 2359328 | tf_op jit(solution)/shard_map/all_to_all | solution.py:75
  426.4 4.3 reshape.90
  430.7 8.1 %gather_fusion.3 = bf16[1024,1024]{1,0:T(8,128)(2,1)} fusion(bf16[1152,1024]{1,0:T(8,128)(2,1)} %reshape.90, s32[1024]{0:T(1024)S(1)} %broadcast_clamp_fusion), kind=kCustom, calls=%fused_computation.3 | custom fusion | bytes 4198400 | tf_op jit(solution)/shard_map/gather | solution.py:87
  (65 shorter events, 25.3 us)
Async XLA Ops:
  7.2 129.9 %copy-start = (bf16[1,1024,768]{2,1,0:T(8,128)(2,1)S(1)}, bf16[1,1024,768]{2,1,0:T(8,128)(2,1)}, u32[]{:S(2)}) copy-start(bf16[1,1024,768]{2,1,0:T(8,128)(2,1)} %param.11) | copy-start | bytes 4718596
  7.2 25.1 %copy-start.10 = (bf16[128,1024]{1,0:T(8,128)(2,1)S(1)}, bf16[128,1024]{1,0:T(8,128)(2,1)}, u32[]{:S(2)}) copy-start(bf16[128,1024]{1,0:T(8,128)(2,1)} %param.7) | copy-start | bytes 786436
  41.5 11.6 %copy-start.12 = (f32[128,8]{0,1:T(8,128)S(1)}, f32[128,8]{0,1:T(8,128)}, u32[]{:S(2)}) copy-start(f32[128,8]{0,1:T(8,128)} %param.10) | copy-start | bytes 12292
  41.5 83.1 %all-to-all-start.1 = ((bf16[64,18,1024]{2,1,0:T(8,128)(2,1)}), bf16[64,18,1024]{2,1,0:T(8,128)(2,1)}, u32[]{:S(2)}, u32[]{:S(2)}) async-start(bf16[64,18,1024]{2,1,0:T(8,128)(2,1)} %reshape.87), calls=%async_computation.1 | async-start | bytes 6291456 | tf_op jit(solution)/shard_map/all_to_all | solution.py:60
  53.4 6.6 %copy-start.11 = (bf16[128,1024]{1,0:T(8,128)(2,1)S(1)}, bf16[128,1024]{1,0:T(8,128)(2,1)}, u32[]{:S(2)}) copy-start(bf16[128,1024]{1,0:T(8,128)(2,1)} %param.8) | copy-start | bytes 786436
  124.6 79.3 %all-to-all-start = ((bf16[64,18,1024]{2,1,0:T(8,128)(2,1)}), bf16[64,18,1024]{2,1,0:T(8,128)(2,1)}, u32[]{:S(2)}, u32[]{:S(2)}) async-start(bf16[64,18,1024]{2,1,0:T(8,128)(2,1)} %multiply_convert_fusion), calls=%async_computation | async-start | bytes 6291456 | tf_op jit(solution)/shard_map/all_to_all | solution.py:61
  132.5 196.0 %all-reduce.5.cloned.1.call-start = ((), (), s32[]{:S(2)}) async-start(), calls=%async_computation.3 | async-start | bytes 10616832 | tf_op jit(solution)/shard_map/psum | solution.py:70
  137.1 5.0 %copy-start.2 = (bf16[1152,1024]{1,0:T(8,128)(2,1)S(1)}, bf16[1152,1024]{1,0:T(8,128)(2,1)}, u32[]{:S(2)}) copy-start(bf16[1152,1024]{1,0:T(8,128)(2,1)} %reshape.88) | copy-start | bytes 7077892
  137.1 5.0 %copy-start.14 = (bf16[1,1024,768]{2,1,0:T(8,128)(2,1)S(1)}, bf16[1,1024,768]{2,1,0:T(8,128)(2,1)}, u32[]{:S(2)}) copy-start(bf16[1,1024,768]{2,1,0:T(8,128)(2,1)} %param.12) | copy-start | bytes 4718596
  145.3 63.0 %copy-start.13 = (bf16[1,768,1024]{2,1,0:T(8,128)(2,1)S(1)}, bf16[1,768,1024]{2,1,0:T(8,128)(2,1)}, u32[]{:S(2)}) copy-start(bf16[1,768,1024]{2,1,0:T(8,128)(2,1)} %param.13) | copy-start | bytes 4718596
  332.6 1.3 copy-start.9
  333.9 2.0 copy-start.5
  333.9 2.1 copy-start.6
  333.9 2.5 copy-start.15
  344.4 82.0 %all-to-all-start.2 = ((bf16[64,18,1024]{2,1,0:T(8,128)(2,1)}), bf16[64,18,1024]{2,1,0:T(8,128)(2,1)}, u32[]{:S(2)}, u32[]{:S(2)}) async-start(bf16[64,18,1024]{2,1,0:T(8,128)(2,1)} %reshape.89), calls=%async_computation.2 | async-start | bytes 6291456 | tf_op jit(solution)/shard_map/all_to_all | solution.py:75
  355.0 5.8 %copy-start.4 = (bf16[1152,1024]{1,0:T(8,128)(2,1)S(1)}, bf16[1152,1024]{1,0:T(8,128)(2,1)}, u32[]{:S(2)}) copy-start(bf16[1152,1024]{1,0:T(8,128)(2,1)} %reshape.86) | copy-start | bytes 7077892
  355.0 5.8 %copy-start.7 = (bf16[1152,768]{1,0:T(8,128)(2,1)S(1)}, bf16[1152,768]{1,0:T(8,128)(2,1)}, u32[]{:S(2)}) copy-start(bf16[1152,768]{1,0:T(8,128)(2,1)} %get-tuple-element.6) | copy-start | bytes 5308420
  355.0 5.8 %copy-start.8 = (bf16[1152,768]{1,0:T(8,128)(2,1)S(1)}, bf16[1152,768]{1,0:T(8,128)(2,1)}, u32[]{:S(2)}) copy-start(bf16[1152,768]{1,0:T(8,128)(2,1)} %get-tuple-element.4) | copy-start | bytes 5308420
  360.8 3.9 copy-start.3
  430.7 11.9 %copy-start.1 = (bf16[1,1024,768]{2,1,0:T(8,128)(2,1)S(1)}, bf16[1,1024,768]{2,1,0:T(8,128)(2,1)}, u32[]{:S(2)}) copy-start(bf16[1,1024,768]{2,1,0:T(8,128)(2,1)} %param.11) | copy-start | bytes 4718596
Sparse Core Ops, SparseCore 0:
  213.5 114.9 all-reduce.4
where the time goes:
time: 453 us; the launch traced here: 449 us
  waiting for transfers between devices  282 us (62%)
  local copies, waits for them, and re-layouts  59.1 us (13%)
  matrix products  32.4 us (7%)
  other arithmetic  31.8 us (7%)
  starting transfers between devices  30.3 us (7%)
  between operations  14.3 us (3%)
    psum x1, waiting for transfers between devices, on_device(): lax.psum(up_part.astype(jnp.bfloat16), 'tp').astype(jnp.float32)  115 us
    all_to_all x1, waiting for transfers between devices, on_device(): lax.all_to_all(send_dy, 'ep', split_axis=0, concat_axis=0, tiled=True)  58.6 us
    all_to_all x1, waiting for transfers between devices, on_device(): lax.all_to_all(dx_rows.reshape(experts, capacity, width_part), 'ep', spli...  58 us
    all_to_all x1, waiting for transfers between devices, on_device(): lax.all_to_all(send_x, 'ep', split_axis=0, concat_axis=0, tiled=True)  49.8 us
    another operation x3, other arithmetic  18.2 us
    dot_general x3, matrix products, contract_rows(): lax.dot_general(left, right, (((0,), (0,)), ((), ())), preferred_element_...  13.4 us
    all_to_all x1, starting transfers between devices, on_device(): lax.all_to_all(send_x, 'ep', split_axis=0, concat_axis=0, tiled=True)  11.6 us
    dot_general x3, matrix products, contract_cols(): lax.dot_general(left, right, (((1,), (1,)), ((), ())), preferred_element_...  10.7 us
  transfers between devices with their start and end apart: 4, of which 4 were waited for; matrix products, arithmetic and copies ran while one was open for 11% of the time, Pallas kernels for 0%

commit v1 on v0

v1 whole, which is shorter than its diff:
```python
import functools

import jax
import jax.numpy as jnp
from jax import lax
from jax.experimental import pallas as pl
from jax.experimental.pallas import tpu as pltpu
from jax.sharding import PartitionSpec as P

BF = jnp.bfloat16
F32 = jnp.float32
GROUP = 8
META = 16
VMEM = 100 * 1024 * 1024 // 2
CHUNKS = ((0, -1, 1), (-2, 2), (-3, 3, 4))


def dot(left, right, dims):
    return lax.dot_general(left, right, ((dims[0], dims[1]), ((), ())), preferred_element_type=F32)


def call(body, outs, args, name, grid=(1,), in_specs=None, out_specs=None, prefetch=0, scratch=()):
    whole = lambda a: pl.BlockSpec(a.shape, lambda *_: (0,) * len(a.shape))
    ins = args[prefetch:]
    in_specs = [whole(a) if s is None else s for a, s in zip(ins, in_specs or [None] * len(ins))]
    out_specs = [whole(a) if s is None else s for a, s in zip(outs, out_specs or [None] * len(outs))]
    return pl.pallas_call(
        body,
        out_shape=outs,
        grid_spec=pltpu.PrefetchScalarGridSpec(
            num_scalar_prefetch=prefetch,
            grid=grid,
            in_specs=in_specs,
            out_specs=out_specs,
            scratch_shapes=scratch,
        ),
        compiler_params=pltpu.CompilerParams(
            dimension_semantics=("arbitrary",) * len(grid), vmem_limit_bytes=VMEM
        ),
        name=name,
    )(*args)


def payload_body(tok, grad, ids, probs, out):
    rows = tok.shape[0]
    out[0:rows, :] = tok[...]
    out[rows : 2 * rows, :] = grad[...]
    p = probs[...]
    high = p.astype(BF).astype(F32)
    mid = (p - high).astype(BF).astype(F32)
    low = p - high - mid
    pad = jnp.zeros((META - p.shape[0], p.shape[1]), F32)
    parts = [jnp.concatenate([v, pad], 0) for v in (ids[...].astype(F32), high, mid, low)]
    used = sum(v.shape[1] for v in parts)
    parts.append(jnp.zeros((META, out.shape[1] - used), F32))
    out[2 * rows :, :] = jnp.concatenate(parts, 1).astype(BF)


def pick_body(cap, place, *refs):
    pays, (send, pick) = refs[:-2], refs[-2:]
    count = len(pays)
    rows = (pays[0].shape[0] - META) // 2
    width = pays[0].shape[1]
    per = pick.shape[0] // GROUP
    first = place[0] // GROUP * GROUP
    before = (
        lax.broadcasted_iota(jnp.int32, (rows, rows), 0) < lax.broadcasted_iota(jnp.int32, (rows, rows), 1)
    ).astype(F32).astype(BF)
    expert = (lax.broadcasted_iota(jnp.int32, (GROUP, GROUP, rows), 0) + first).astype(F32)
    codes, probs = [], []
    for at, pay in enumerate(pays):
        meta = pay[2 * rows :, : 4 * rows].astype(F32)[:GROUP]
        ids, p = meta[:, :rows], meta[:, rows : 2 * rows] + meta[:, 2 * rows : 3 * rows] + meta[:, 3 * rows :]
        named = expert == ids[None]
        has = jnp.sum(jnp.where(named, 1.0, 0.0), 1)
        probs.append(jnp.sum(jnp.where(named, p[None], 0.0), 1))
        rank = dot(has.astype(BF), before, ((1,), (0,)))
        codes.append(jnp.where(has > 0.5, rank + 32.0 * at, -1.0))
    codes, probs = jnp.concatenate(codes, 1), jnp.concatenate(probs, 1)
    row = lax.broadcasted_iota(jnp.int32, (per, count * rows), 0)
    code = row
    for at in range(count):
        code = code + jnp.where(row >= cap * (at + 1), 32 - cap, 0)
    code = code.astype(F32)
    scales = []
    for d in range(GROUP):
        hit = code == codes[d : d + 1]
        pick[d * per : (d + 1) * per, :] = jnp.where(hit, 1.0, 0.0).astype(BF)
        scales.append(jnp.sum(jnp.where(hit, probs[d : d + 1], 0.0), 1, keepdims=True))
    onehot = pick[...]
    toks = jnp.concatenate([pay[0:rows, :] for pay in pays], 0)
    send[:, :width] = dot(onehot, toks, ((1,), (0,))).astype(BF)
    grads = jnp.concatenate([pay[rows : 2 * rows, :] for pay in pays], 0)
    send[:, width:] = (dot(onehot, grads, ((1,), (0,))) * jnp.concatenate(scales, 0)).astype(BF)


def partial_body(side, rows_ref, gate, up, down, send, keep, work):
    half = send.shape[1]
    width = gate.shape[1]
    kept = pl.multiple_of(side[0] * half, 16)
    sent = pl.multiple_of((1 - side[0]) * half, 16)
    for at in range(3):
        if at < 2:
            work[...] = dot(rows_ref[:, :width], (gate, up)[at][0], ((1,), (0,)))
        else:
            work[...] = dot(rows_ref[:, width:], down[0], ((1,), (1,)))
        send[at] = work[pl.ds(sent, half), :].astype(BF)
        keep[at] = work[pl.ds(kept, half), :].astype(BF)


def pair_body(side, keep, got, out):
    out[...] = (keep[...].astype(F32) + got[...].astype(F32)).astype(BF)


def back_body(side, keep, got, more, out):
    gate, up, dact = (keep[i].astype(F32) + got[i].astype(F32) + more[i].astype(F32) for i in range(3))
    sig = 1.0 / (1.0 + jnp.exp(-gate))
    out[0] = (gate * sig * up).astype(BF)
    out[1] = (dact * up * sig * (1.0 + gate * (1.0 - sig))).astype(BF)
    out[2] = (dact * gate * sig).astype(BF)


def input_body(side, own, near, far, last, gate, up, out, sq, work):
    quarter = own.shape[1]

    @pl.when(pl.program_id(0) == 0)
    def _():
        h, q = side[0], side[1]
        places = (2 * h + q, 2 * h + 1 - q, 2 * (1 - h) + q, 2 * (1 - h) + 1 - q)
        for place, ref in zip(places, (own, near, far, last)):
            at = pl.ds(pl.multiple_of(place * quarter, 16), quarter)
            for i in range(3):
                v = ref[i].astype(F32)
                sq[i, at, :] = (v * v).astype(BF)
                if i:
                    work[i - 1, at, :] = ref[i]

    out[...] = (dot(work[0], gate[0], ((1,), (1,))) + dot(work[1], up[0], ((1,), (1,)))).astype(BF)


def square_bf(values):
    v = values.astype(F32)
    return (v * v).astype(BF)


def fisher_body(scale, *refs):
    count = (len(refs) - 5) // 2
    rows, sqs = refs[:count], refs[count : 2 * count]
    f_gate, f_up, f_down, x_sq, dy_sq = refs[2 * count :]
    width = x_sq.shape[1]

    @pl.when(pl.program_id(0) == 0)
    def _():
        at = 0
        for ref in rows:
            x_sq[at : at + ref.shape[0], :] = square_bf(ref[:, :width])
            dy_sq[at : at + ref.shape[0], :] = square_bf(ref[:, width:])
            at += ref.shape[0]

    act, dgate, dup = (jnp.concatenate([s[i] for s in sqs], 0) for i in range(3))
    f_gate[0] = (dot(x_sq[...], dgate, ((0,), (0,))) * scale).astype(BF)
    f_up[0] = (dot(x_sq[...], dup, ((0,), (0,))) * scale).astype(BF)
    f_down[0] = (dot(act, dy_sq[...], ((0,), (0,))) * scale).astype(BF)


def combine_body(pick, got, *outs):
    rows = outs[0].shape[0]
    for at, out in enumerate(outs):
        out[...] = dot(pick[:, at * rows : (at + 1) * rows], got[...], ((0,), (0,))).astype(out.dtype)


def total_body(*refs):
    total = refs[0][...].astype(F32)
    for ref in refs[1:-1]:
        total = total + ref[...].astype(F32)
    refs[-1][...] = total.astype(BF)


def shape(dims, dtype=BF):
    return jax.ShapeDtypeStruct(dims, dtype)


def on_device(tokens, out_grad, expert_ids, route_probs, w_gate, w_up, w_down):
    rows, width = tokens.shape
    top = expert_ids.shape[1]
    ep, tp = lax.axis_size("ep"), lax.axis_size("tp")
    hidden = w_gate.shape[2]
    cap = rows * top * 9 // (8 * ep)
    deep = ep // GROUP
    groups = [[z * GROUP + i for i in range(GROUP)] for z in range(deep)]

    def along_z(value, step):
        n = ep * tp
        return lax.ppermute(value, ("ep", "tp"), [(i, (i + step * GROUP * tp) % n) for i in range(n)])

    def along_x(value, which):
        pairs = []
        for i in range(ep * tp):
            e, x = divmod(i, tp)
            pairs.append((i, e * tp + (x ^ 1 if (e % 2 == 0) == (which == 1) else 3 - x)))
        return lax.ppermute(value, ("ep", "tp"), pairs)

    def across(value):
        split = value.reshape(GROUP, -1, value.shape[1])
        return lax.all_to_all(
            split, "ep", split_axis=0, concat_axis=0, axis_index_groups=groups, tiled=True
        ).reshape(value.shape)

    e, x = lax.axis_index("ep"), lax.axis_index("tp")
    place = e.astype(jnp.int32).reshape(1)
    outer = (x ^ (x >> 1)) & 1
    upper = x >> 1
    even = e % 2 == 0
    side = jnp.stack([jnp.where(even, outer, upper), jnp.where(even, upper, outer)]).astype(jnp.int32)

    pays = {}
    (pays[0],) = call(
        payload_body,
        [shape((2 * rows + META, width))],
        [tokens, out_grad, expert_ids.T, route_probs.T],
        "payload",
    )
    for step in range(1, deep // 2):
        pays[-step] = along_z(pays[1 - step], 1)
        pays[step] = along_z(pays[step - 1], -1)
    pays[deep // 2] = along_z(pays[1 - deep // 2], 1)

    tile = 256
    steps = hidden // tile
    picks, recvs, sqs, parts = [], [], [], []
    for offsets in CHUNKS:
        count = len(offsets)
        per = -(-count * cap // 8) * 8
        total = GROUP * per
        half, quarter = total // 2, total // 4
        send, pick = call(
            functools.partial(pick_body, cap),
            [shape((total, 2 * width)), shape((total, count * rows))],
            [place] + [pays[o] for o in offsets],
            "pick",
            prefetch=1,
        )
        recv = across(send)
        w_in = pl.BlockSpec((1, width, tile), lambda j, s: (0, 0, j))
        half_out = pl.BlockSpec((3, half, tile), lambda j, s: (0, 0, j))
        give, keep = call(
            partial_body,
            [shape((3, half, hidden))] * 2,
            [side, recv, w_gate, w_up, w_down],
            "partial",
            grid=(steps,),
            in_specs=[None, w_in, w_in, pl.BlockSpec((1, tile, width), lambda j, s: (0, j, 0))],
            out_specs=[half_out, half_out],
            prefetch=1,
            scratch=[pltpu.VMEM((total, tile), F32)],
        )
        got = along_x(give, 1)
        theirs = pl.BlockSpec((3, quarter, hidden), lambda j, s: (0, 1 - s[1], 0))
        mine = pl.BlockSpec((3, quarter, hidden), lambda j, s: (0, s[1], 0))
        quarters = shape((3, quarter, hidden))
        (give,) = call(pair_body, [quarters], [side, keep, got], "pair", in_specs=[theirs, theirs], prefetch=1)
        more = along_x(give, 2)
        (own,) = call(
            back_body, [quarters], [side, keep, got, more], "back", in_specs=[mine, mine, None], prefetch=1
        )
        near = along_x(own, 2)
        far = along_x(own, 1)
        last = along_x(near, 1)
        w_out = pl.BlockSpec((1, tile, hidden), lambda j, s: (0, j, 0))
        d_rows, sq = call(
            input_body,
            [shape((total, width)), shape((3, total, hidden))],
            [side, own, near, far, last, w_gate, w_up],
            "input_grad",
            grid=(width // tile,),
            in_specs=[None] * 4 + [w_out, w_out],
            out_specs=[pl.BlockSpec((total, tile), lambda j, s: (0, j)), None],
            prefetch=1,
            scratch=[pltpu.VMEM((2, total, hidden), BF)],
        )
        back = across(d_rows)
        sums = call(
            combine_body,
            [shape((rows, width), BF if o else F32) for o in offsets],
            [pick, back],
            "combine",
        )
        for o, s in zip(offsets, sums):
            parts.append(along_z(s, o) if o else s)
        recvs.append(recv)
        sqs.append(sq)
    (grad_tokens,) = call(total_body, [shape((rows, width))], parts, "total")
    every = sum(r.shape[0] for r in recvs)
    f_in = pl.BlockSpec((1, width, tile), lambda j: (0, 0, j))
    fishers = call(
        functools.partial(fisher_body, 1.0 / rows),
        [shape((1, width, hidden)), shape((1, width, hidden)), shape((1, hidden, width))],
        recvs + sqs,
        "fisher",
        grid=(steps,),
        in_specs=[None] * len(recvs)
        + [pl.BlockSpec((3, s.shape[1], tile), lambda j: (0, 0, j)) for s in sqs],
        out_specs=[f_in, f_in, pl.BlockSpec((1, tile, width), lambda j: (0, j, 0))],
        scratch=[pltpu.VMEM((every, width), BF)] * 2,
    )
    return (grad_tokens, *fishers)


def solution(mesh):
    in_specs = (
        P("ep", "tp"),
        P("ep", "tp"),
        P("ep", None),
        P("ep", None),
        P("ep", "tp", None),
        P("ep", "tp", None),
        P("ep", None, "tp"),
    )
    out_specs = (P("ep", "tp"), P("ep", "tp", None), P("ep", "tp", None), P("ep", None, "tp"))
    return jax.shard_map(
        on_device, mesh=mesh, in_specs=in_specs, out_specs=out_specs, check_vma=False
    )
```

time: 453 us -> 300 us (0.66)
  waiting for transfers between devices: 282 us -> 142 us
  Pallas kernels: 0 us -> 69.5 us
  local copies, waits for them, and re-layouts: 59.1 us -> 15 us
  starting transfers between devices: 30.3 us -> 70.4 us
  matrix products: 32.4 us -> 0 us
  other arithmetic: 31.8 us -> 0.08 us
  between operations: 14.3 us -> 0.84 us
    all_to_all x3 -> x6, waiting for transfers between devices: 166 us -> 19.3 us  [across(): lax.all_to_all(split, 'ep', split_axis=0, concat_axis=0, axis_index_group...]
    ppermute x0 -> x29, waiting for transfers between devices: none -> 123 us  [the longest x14 70.9 us: along_z(): lax.ppermute(value, ('ep', 'tp'), [(i, (i + step * GROUP * tp) % n) for i...]
    psum x1 -> x0, waiting for transfers between devices: 115 us -> none  [on_device(): lax.psum(up_part.astype(jnp.bfloat16), 'tp').astype(jnp.float32)]
    pallas_call x0 -> x21, Pallas kernels: none -> 69.5 us  [call(): pl.pallas_call(body, out_shape=outs, grid_spec=pltpu.PrefetchScalarGridSp...]
    ppermute x0 -> x29, starting transfers between devices: none -> 44.5 us  [the longest x14 24.9 us: along_z(): lax.ppermute(value, ('ep', 'tp'), [(i, (i + step * GROUP * tp) % n) for i...]
    dot_general x8 -> x0, matrix products: 32.4 us -> none  [the longest x3 13.4 us: contract_rows(): lax.dot_general(left, right, (((0,), (0,)), ((), ())), preferred_element_...]
    gather x4 -> x0, local copies, waits for them, and re-layouts: 24.6 us -> none  [the longest x1 8.15 us: on_device(): returned.reshape(experts * capacity, width_part)[slot_index]]
    reshape x6 -> x0, local copies, waits for them, and re-layouts: 21.8 us -> none  [the longest x1 4.4 us: on_device(): recv_dy = recv_dy.reshape(-1, width_part)]
  transfers between devices with their start and end apart: 4 -> 35, of which waited for: 4 -> 19; matrix products, arithmetic and copies ran while one was open for 11% -> 0% of each run, Pallas kernels for 0% -> 22%
where the time goes in v1:
time: 300 us; the launch traced here: 298 us
  waiting for transfers between devices  142 us (47%)
  starting transfers between devices  70.4 us (23%)
  Pallas kernels  69.5 us (23%)
  local copies, waits for them, and re-layouts  15 us (5%)
    ppermute x14, waiting for transfers between devices, along_z(): lax.ppermute(value, ('ep', 'tp'), [(i, (i + step * GROUP * tp) % n) for i...  70.9 us
    pallas_call x21, Pallas kernels, call(): pl.pallas_call(body, out_shape=outs, grid_spec=pltpu.PrefetchScalarGridSp...  69.5 us
    ppermute x15, waiting for transfers between devices, along_x(): return lax.ppermute(value, ('ep', 'tp'), pairs)  52.1 us
    all_to_all x6, starting transfers between devices, across(): lax.all_to_all(split, 'ep', split_axis=0, concat_axis=0, axis_index_group...  25.9 us
    ppermute x14, starting transfers between devices, along_z(): lax.ppermute(value, ('ep', 'tp'), [(i, (i + step * GROUP * tp) % n) for i...  24.9 us
    ppermute x15, starting transfers between devices, along_x(): return lax.ppermute(value, ('ep', 'tp'), pairs)  19.5 us
    all_to_all x6, waiting for transfers between devices, across(): lax.all_to_all(split, 'ep', split_axis=0, concat_axis=0, axis_index_group...  19.3 us
    unnamed x52, local copies, waits for them, and re-layouts  15 us
  transfers between devices with their start and end apart: 35, of which 19 were waited for; matrix products, arithmetic and copies ran while one was open for 0% of the time, Pallas kernels for 22%

profile of v1, /device:TPU:64, one launch (start us, length us, event | category | flops | bytes accessed | tf_op | source)
XLA Modules:
  0.0 298.2 jit_solution(13666955479453907829)
XLA Ops:
  6.1 12.3 %collective-permute-done.refs_1_ = bf16[272,1024]{1,0:T(8,128)(2,1)S(1)} collective-permute-done((bf16[272,1024]{1,0:T(8,128)(2,1)S(1)}, bf16[272,1024]{1,0:T(8,128)(2,1)S(1)}, u32[]{:S(2)}, u32[]{:S(2)}) %collective-permute-start) | collective-permute-done | bytes 557088 | tf_op jit(solution)/shard_map/ppermute | solution.py:194
  24.7 4.5 %all-to-all-start = ((bf16[8,56,2048]{2,1,0:T(8,128)(2,1)}), bf16[8,56,2048]{2,1,0:T(8,128)(2,1)}, u32[]{:S(2)}, u32[]{:S(2)}) async-start(bf16[8,56,2048]{2,1,0:T(8,128)(2,1)} %bitcast.5), calls=%async_computation | async-start | bytes 3670016 | tf_op jit(solution)/shard_map/all_to_all | solution.py:205
  32.2 12.5 %collective-permute-done.9.refs_0_ = bf16[272,1024]{1,0:T(8,128)(2,1)S(1)} collective-permute-done((bf16[272,1024]{1,0:T(8,128)(2,1)S(1)}, bf16[272,1024]{1,0:T(8,128)(2,1)S(1)}, u32[]{:S(2)}, u32[]{:S(2)}) %collective-permute-start.9) | collective-permute-done | bytes 557088 | tf_op jit(solution)/shard_map/ppermute | solution.py:194
  60.3 12.4 %collective-permute-done.18.refs_0_ = bf16[272,1024]{1,0:T(8,128)(2,1)S(1)} collective-permute-done((bf16[272,1024]{1,0:T(8,128)(2,1)S(1)}, bf16[272,1024]{1,0:T(8,128)(2,1)S(1)}, u32[]{:S(2)}, u32[]{:S(2)}) %collective-permute-start.18) | collective-permute-done | bytes 557088 | tf_op jit(solution)/shard_map/ppermute | solution.py:194
  75.2 11.6 %collective-permute-done.20.refs_2_ = bf16[272,1024]{1,0:T(8,128)(2,1)S(1)} collective-permute-done((bf16[272,1024]{1,0:T(8,128)(2,1)S(1)}, bf16[272,1024]{1,0:T(8,128)(2,1)S(1)}, u32[]{:S(2)}, u32[]{:S(2)}) %collective-permute-start.20) | collective-permute-done | bytes 557088 | tf_op jit(solution)/shard_map/ppermute | solution.py:194
  94.6 6.4 %partial.3 = (bf16[3,224,768]{2,1,0:T(8,128)(2,1)}, bf16[3,224,768]{2,1,0:T(8,128)(2,1)S(1)}) custom-call(s32[2]{0:T(128)S(1)} %pad_add_fusion.side, bf16[448,2048]{1,0:T(8,128)(2,1)} %bitcast.6.rows_ref.refs_0_, bf16[1,1024,768]{2,1,0:T(8,128)(2,1)S(1)} %copy-done, bf16[1,1024,768]{2,1,0:T(8,128)(2,1)} %up.11, bf16[1,768,1024]{2,1,0:T(8,128)(2,1)} %down.5), custom_call_target="tpu_custom_call" | custom-call | tf_op jit(solution)/shard_map/partial/pallas_call | solution.py:27
  102.5 5.6 %partial.4 = (bf16[3,160,768]{2,1,0:T(8,128)(2,1)}, bf16[3,160,768]{2,1,0:T(8,128)(2,1)S(1)}) custom-call(s32[2]{0:T(128)S(1)} %pad_add_fusion.side, bf16[320,2048]{1,0:T(8,128)(2,1)S(1)} %bitcast.17, bf16[1,1024,768]{2,1,0:T(8,128)(2,1)} %gate.11, bf16[1,1024,768]{2,1,0:T(8,128)(2,1)} %up.11, bf16[1,768,1024]{2,1,0:T(8,128)(2,1)} %down.5), custom_call_target="tpu_custom_call" | custom-call | tf_op jit(solution)/shard_map/partial/pallas_call | solution.py:27
  109.6 9.4 %all-to-all-done.4 = bf16[8,56,2048]{2,1,0:T(8,128)(2,1)} async-done(((bf16[8,56,2048]{2,1,0:T(8,128)(2,1)}), bf16[8,56,2048]{2,1,0:T(8,128)(2,1)}, u32[]{:S(2)}, u32[]{:S(2)}) %all-to-all-start.4) | async-done | bytes 1835040 | tf_op jit(solution)/shard_map/all_to_all | solution.py:205
  118.9 5.7 %partial.5 = (bf16[3,224,768]{2,1,0:T(8,128)(2,1)S(1)}, bf16[3,224,768]{2,1,0:T(8,128)(2,1)S(1)}) custom-call(s32[2]{0:T(128)S(1)} %pad_add_fusion.side, bf16[448,2048]{1,0:T(8,128)(2,1)} %bitcast.14.rows_ref.refs_2_, bf16[1,1024,768]{2,1,0:T(8,128)(2,1)S(1)} %copy-done.1, bf16[1,1024,768]{2,1,0:T(8,128)(2,1)} %up.11, bf16[1,768,1024]{2,1,0:T(8,128)(2,1)} %down.5), custom_call_target="tpu_custom_call" | custom-call | tf_op jit(solution)/shard_map/partial/pallas_call | solution.py:27
  133.1 7.7 %collective-permute-done.12.more = bf16[3,80,768]{2,1,0:T(8,128)(2,1)S(1)} collective-permute-done((bf16[3,80,768]{2,1,0:T(8,128)(2,1)S(1)}, bf16[3,80,768]{2,1,0:T(8,128)(2,1)S(1)}, u32[]{:S(2)}, u32[]{:S(2)}) %collective-permute-start.12) | collective-permute-done | bytes 368672 | tf_op jit(solution)/shard_map/ppermute | solution.py:201
  157.6 7.5 %collective-permute-done.14.far = bf16[3,80,768]{2,1,0:T(8,128)(2,1)S(1)} collective-permute-done((bf16[3,80,768]{2,1,0:T(8,128)(2,1)S(1)}, bf16[3,80,768]{2,1,0:T(8,128)(2,1)S(1)}, u32[]{:S(2)}, u32[]{:S(2)}) %collective-permute-start.14) | collective-permute-done | bytes 368672 | tf_op jit(solution)/shard_map/ppermute | solution.py:201
  165.1 7.5 %collective-permute-done.15.last = bf16[3,80,768]{2,1,0:T(8,128)(2,1)S(1)} collective-permute-done((bf16[3,80,768]{2,1,0:T(8,128)(2,1)S(1)}, bf16[3,80,768]{2,1,0:T(8,128)(2,1)S(1)}, u32[]{:S(2)}, u32[]{:S(2)}) %collective-permute-start.15) | collective-permute-done | bytes 368672 | tf_op jit(solution)/shard_map/ppermute | solution.py:201
  172.6 4.6 %input_grad.4 = (bf16[320,1024]{1,0:T(8,128)(2,1)S(1)}, bf16[3,320,768]{2,1,0:T(8,128)(2,1)S(1)}) custom-call(s32[2]{0:T(128)S(1)} %pad_add_fusion.side, bf16[3,80,768]{2,1,0:T(8,128)(2,1)S(1)} %back.4.own, bf16[3,80,768]{2,1,0:T(8,128)(2,1)S(1)} %collective-permute-done.13.near, bf16[3,80,768]{2,1,0:T(8,128)(2,1)S(1)} %collective-permute-done.14.far, ...), custom_call_target="tpu_custom_call" | custom-call | tf_op jit(solution)/shard_map/input_grad/pallas_call | solution.py:27
  192.1 10.3 %collective-permute-done.6.last = bf16[3,112,768]{2,1,0:T(8,128)(2,1)S(1)} collective-permute-done((bf16[3,112,768]{2,1,0:T(8,128)(2,1)}, bf16[3,112,768]{2,1,0:T(8,128)(2,1)S(1)}, u32[]{:S(2)}, u32[]{:S(2)}) %collective-permute-start.6) | collective-permute-done | bytes 516128 | tf_op jit(solution)/shard_map/ppermute | solution.py:201
  202.4 6.5 %input_grad.3 = (bf16[448,1024]{1,0:T(8,128)(2,1)S(1)}, bf16[3,448,768]{2,1,0:T(8,128)(2,1)}) custom-call(s32[2]{0:T(128)S(1)} %pad_add_fusion.side, bf16[3,112,768]{2,1,0:T(8,128)(2,1)S(1)} %back.3.own, bf16[3,112,768]{2,1,0:T(8,128)(2,1)} %collective-permute-done.4.near, bf16[3,112,768]{2,1,0:T(8,128)(2,1)S(1)} %collective-permute-done.5.far, ...), custom_call_target="tpu_custom_call" | custom-call | tf_op jit(solution)/shard_map/input_grad/pallas_call | solution.py:27
  209.8 4.8 %all-to-all-start.1 = ((bf16[8,56,1024]{2,1,0:T(8,128)(2,1)}), bf16[8,56,1024]{2,1,0:T(8,128)(2,1)S(1)}, u32[]{:S(2)}, u32[]{:S(2)}) async-start(bf16[8,56,1024]{2,1,0:T(8,128)(2,1)} %bitcast.23), calls=%async_computation.1 | async-start | bytes 1835008 | tf_op jit(solution)/shard_map/all_to_all | solution.py:205
  216.7 7.3 %collective-permute-done.24.far = bf16[3,112,768]{2,1,0:T(8,128)(2,1)S(1)} collective-permute-done((bf16[3,112,768]{2,1,0:T(8,128)(2,1)}, bf16[3,112,768]{2,1,0:T(8,128)(2,1)S(1)}, u32[]{:S(2)}, u32[]{:S(2)}) %collective-permute-start.24) | collective-permute-done | bytes 516128 | tf_op jit(solution)/shard_map/ppermute | solution.py:201
  223.9 5.5 %collective-permute-done.25.last = bf16[3,112,768]{2,1,0:T(8,128)(2,1)S(1)} collective-permute-done((bf16[3,112,768]{2,1,0:T(8,128)(2,1)S(1)}, bf16[3,112,768]{2,1,0:T(8,128)(2,1)S(1)}, u32[]{:S(2)}, u32[]{:S(2)}) %collective-permute-start.25) | collective-permute-done | bytes 516128 | tf_op jit(solution)/shard_map/ppermute | solution.py:201
  229.5 6.5 %input_grad.5 = (bf16[448,1024]{1,0:T(8,128)(2,1)S(1)}, bf16[3,448,768]{2,1,0:T(8,128)(2,1)}) custom-call(s32[2]{0:T(128)S(1)} %pad_add_fusion.side, bf16[3,112,768]{2,1,0:T(8,128)(2,1)} %back.5.own, bf16[3,112,768]{2,1,0:T(8,128)(2,1)S(1)} %collective-permute-done.23.near, bf16[3,112,768]{2,1,0:T(8,128)(2,1)S(1)} %collective-permute-done.24.far, ...), custom_call_target="tpu_custom_call" | custom-call | tf_op jit(solution)/shard_map/input_grad/pallas_call | solution.py:27
  236.9 4.9 %all-to-all-start.5 = ((bf16[8,56,1024]{2,1,0:T(8,128)(2,1)}), bf16[8,56,1024]{2,1,0:T(8,128)(2,1)}, u32[]{:S(2)}, u32[]{:S(2)}) async-start(bf16[8,56,1024]{2,1,0:T(8,128)(2,1)} %bitcast.22), calls=%async_computation.5 | async-start | bytes 1835008 | tf_op jit(solution)/shard_map/all_to_all | solution.py:205
  251.0 5.5 %all-to-all-done.5 = bf16[8,56,1024]{2,1,0:T(8,128)(2,1)} async-done(((bf16[8,56,1024]{2,1,0:T(8,128)(2,1)}), bf16[8,56,1024]{2,1,0:T(8,128)(2,1)}, u32[]{:S(2)}, u32[]{:S(2)}) %all-to-all-start.5) | async-done | bytes 917536 | tf_op jit(solution)/shard_map/all_to_all | solution.py:205
  268.4 11.0 %fisher.1 = (bf16[1,1024,768]{2,1,0:T(8,128)(2,1)}, bf16[1,1024,768]{2,1,0:T(8,128)(2,1)}, bf16[1,768,1024]{2,1,0:T(8,128)(2,1)}) custom-call(bf16[448,2048]{1,0:T(8,128)(2,1)} %bitcast.6.rows_ref.refs_0_, bf16[320,2048]{1,0:T(8,128)(2,1)S(1)} %bitcast.18, bf16[448,2048]{1,0:T(8,128)(2,1)} %bitcast.14.rows_ref.refs_2_, ...), custom_call_target="tpu_custom_call" | custom-call | tf_op jit(solution)/shard_map/fisher/pallas_call | solution.py:27
  279.4 6.7 %collective-permute-done.26.refs_5_ = bf16[128,1024]{1,0:T(8,128)(2,1)S(1)} collective-permute-done((bf16[128,1024]{1,0:T(8,128)(2,1)S(1)}, bf16[128,1024]{1,0:T(8,128)(2,1)S(1)}, u32[]{:S(2)}, u32[]{:S(2)}) %collective-permute-start.26) | collective-permute-done | bytes 262176 | tf_op jit(solution)/shard_map/ppermute | solution.py:194
  286.1 10.2 %collective-permute-done.28.refs_7_ = bf16[128,1024]{1,0:T(8,128)(2,1)S(1)} collective-permute-done((bf16[128,1024]{1,0:T(8,128)(2,1)S(1)}, bf16[128,1024]{1,0:T(8,128)(2,1)S(1)}, u32[]{:S(2)}, u32[]{:S(2)}) %collective-permute-start.28) | collective-permute-done | bytes 262176 | tf_op jit(solution)/shard_map/ppermute | solution.py:194
  (120 shorter events, 110.4 us)
Async XLA Ops:
  5.9 15.5 %collective-permute-start.1 = (bf16[272,1024]{1,0:T(8,128)(2,1)S(1)}, bf16[272,1024]{1,0:T(8,128)(2,1)S(1)}, u32[]{:S(2)}, u32[]{:S(2)}) collective-permute-start(bf16[272,1024]{1,0:T(8,128)(2,1)S(1)} %payload.1.refs_0_), channel_id=1, source_target_pairs={{0,224},{1,225},{2,226},{3,227},{4,228},{5,229},{6,230},{7,231},{8... | collective-permute-start | bytes 1671176 | tf_op jit(solution)/shard_map/ppermute | solution.py:194
  24.7 29.0 %all-to-all-start = ((bf16[8,56,2048]{2,1,0:T(8,128)(2,1)}), bf16[8,56,2048]{2,1,0:T(8,128)(2,1)}, u32[]{:S(2)}, u32[]{:S(2)}) async-start(bf16[8,56,2048]{2,1,0:T(8,128)(2,1)} %bitcast.5), calls=%async_computation | async-start | bytes 3670016 | tf_op jit(solution)/shard_map/all_to_all | solution.py:205
  29.2 15.5 %collective-permute-start.9 = (bf16[272,1024]{1,0:T(8,128)(2,1)S(1)}, bf16[272,1024]{1,0:T(8,128)(2,1)S(1)}, u32[]{:S(2)}, u32[]{:S(2)}) collective-permute-start(bf16[272,1024]{1,0:T(8,128)(2,1)S(1)} %collective-permute-done.refs_1_), channel_id=1, source_target_pairs={{0,32},{1,33},{2,34},{3,35},{4,36},{5,37},{6,38},{7,39},{8,40},{9,... | collective-permute-start | bytes 1671176 | tf_op jit(solution)/shard_map/ppermute | solution.py:194
  53.7 36.4 %all-to-all-start.2 = ((bf16[8,40,2048]{2,1,0:T(8,128)(2,1)}), bf16[8,40,2048]{2,1,0:T(8,128)(2,1)S(1)}, u32[]{:S(2)}, u32[]{:S(2)}) async-start(bf16[8,40,2048]{2,1,0:T(8,128)(2,1)} %bitcast.9), calls=%async_computation.2 | async-start | bytes 2621440 | tf_op jit(solution)/shard_map/all_to_all | solution.py:205
  90.0 28.9 %all-to-all-start.4 = ((bf16[8,56,2048]{2,1,0:T(8,128)(2,1)}), bf16[8,56,2048]{2,1,0:T(8,128)(2,1)}, u32[]{:S(2)}, u32[]{:S(2)}) async-start(bf16[8,56,2048]{2,1,0:T(8,128)(2,1)} %bitcast.21), calls=%async_computation.4 | async-start | bytes 3670016 | tf_op jit(solution)/shard_map/all_to_all | solution.py:205
  101.1 29.1 %collective-permute-start.2 = (bf16[3,224,768]{2,1,0:T(8,128)(2,1)}, bf16[3,224,768]{2,1,0:T(8,128)(2,1)}, u32[]{:S(2)}, u32[]{:S(2)}) collective-permute-start(bf16[3,224,768]{2,1,0:T(8,128)(2,1)} %get-tuple-element.36), channel_id=1, source_target_pairs={{0,1},{1,0},{2,3},{3,2},{4,7},{5,6},{6,5},{7,4},{8,9},{9,8},{10,11... | collective-permute-start | bytes 3096584 | tf_op jit(solution)/shard_map/ppermute | solution.py:201
  109.0 17.3 %collective-permute-start.11 = (bf16[3,160,768]{2,1,0:T(8,128)(2,1)}, bf16[3,160,768]{2,1,0:T(8,128)(2,1)}, u32[]{:S(2)}, u32[]{:S(2)}) collective-permute-start(bf16[3,160,768]{2,1,0:T(8,128)(2,1)} %get-tuple-element.44), channel_id=1, source_target_pairs={{0,1},{1,0},{2,3},{3,2},{4,7},{5,6},{6,5},{7,4},{8,9},{9,8},{10,11... | collective-permute-start | bytes 2211848 | tf_op jit(solution)/shard_map/ppermute | solution.py:201
  124.7 30.9 %collective-permute-start.21 = (bf16[3,224,768]{2,1,0:T(8,128)(2,1)S(1)}, bf16[3,224,768]{2,1,0:T(8,128)(2,1)S(1)}, u32[]{:S(2)}, u32[]{:S(2)}) collective-permute-start(bf16[3,224,768]{2,1,0:T(8,128)(2,1)S(1)} %get-tuple-element.51), channel_id=1, source_target_pairs={{0,1},{1,0},{2,3},{3,2},{4,7},{5,6},{6,5},{7,4},{8,9},{9,8},{10,11... | collective-permute-start | bytes 3096584 | tf_op jit(solution)/shard_map/ppermute | solution.py:201
  131.9 16.9 %collective-permute-start.3 = (bf16[3,112,768]{2,1,0:T(8,128)(2,1)S(1)}, bf16[3,112,768]{2,1,0:T(8,128)(2,1)S(1)}, u32[]{:S(2)}, u32[]{:S(2)}) collective-permute-start(bf16[3,112,768]{2,1,0:T(8,128)(2,1)S(1)} %pair.3), channel_id=1, source_target_pairs={{0,3},{1,2},{2,1},{3,0},{4,5},{5,4},{6,7},{7,6},{8,11},{9,10},{10,... | collective-permute-start | bytes 1548296 | tf_op jit(solution)/shard_map/ppermute | solution.py:201
  150.8 32.6 %collective-permute-start.4 = (bf16[3,112,768]{2,1,0:T(8,128)(2,1)S(1)}, bf16[3,112,768]{2,1,0:T(8,128)(2,1)}, u32[]{:S(2)}, u32[]{:S(2)}) collective-permute-start(bf16[3,112,768]{2,1,0:T(8,128)(2,1)S(1)} %back.3.own), channel_id=1, source_target_pairs={{0,3},{1,2},{2,1},{3,0},{4,5},{5,4},{6,7},{7,6},{8,11},{9,10},{10,... | collective-permute-start | bytes 1548296 | tf_op jit(solution)/shard_map/ppermute | solution.py:201
  153.6 19.0 %collective-permute-start.15 = (bf16[3,80,768]{2,1,0:T(8,128)(2,1)S(1)}, bf16[3,80,768]{2,1,0:T(8,128)(2,1)S(1)}, u32[]{:S(2)}, u32[]{:S(2)}) collective-permute-start(bf16[3,80,768]{2,1,0:T(8,128)(2,1)S(1)} %collective-permute-done.13.near), channel_id=1, source_target_pairs={{0,1},{1,0},{2,3},{3,2},{4,7},{5,6},{6,5},{7,4},{8,9},{9,8},{10,11... | collective-permute-start | bytes 1105928 | tf_op jit(solution)/shard_map/ppermute | solution.py:201
  157.1 27.9 %collective-permute-start.22 = (bf16[3,112,768]{2,1,0:T(8,128)(2,1)}, bf16[3,112,768]{2,1,0:T(8,128)(2,1)}, u32[]{:S(2)}, u32[]{:S(2)}) collective-permute-start(bf16[3,112,768]{2,1,0:T(8,128)(2,1)} %pair.5), channel_id=1, source_target_pairs={{0,3},{1,2},{2,1},{3,0},{4,5},{5,4},{6,7},{7,6},{8,11},{9,10},{10,... | collective-permute-start | bytes 1548296 | tf_op jit(solution)/shard_map/ppermute | solution.py:201
  179.2 30.6 %all-to-all-start.3 = ((bf16[8,40,1024]{2,1,0:T(8,128)(2,1)}), bf16[8,40,1024]{2,1,0:T(8,128)(2,1)S(1)}, u32[]{:S(2)}, u32[]{:S(2)}) async-start(bf16[8,40,1024]{2,1,0:T(8,128)(2,1)} %bitcast.24), calls=%async_computation.3 | async-start | bytes 1310720 | tf_op jit(solution)/shard_map/all_to_all | solution.py:205
  183.4 19.0 %collective-permute-start.6 = (bf16[3,112,768]{2,1,0:T(8,128)(2,1)}, bf16[3,112,768]{2,1,0:T(8,128)(2,1)S(1)}, u32[]{:S(2)}, u32[]{:S(2)}) collective-permute-start(bf16[3,112,768]{2,1,0:T(8,128)(2,1)} %collective-permute-done.4.near), channel_id=1, source_target_pairs={{0,1},{1,0},{2,3},{3,2},{4,7},{5,6},{6,5},{7,4},{8,9},{9,8},{10,11... | collective-permute-start | bytes 1548296 | tf_op jit(solution)/shard_map/ppermute | solution.py:201
  189.0 26.1 %collective-permute-start.23 = (bf16[3,112,768]{2,1,0:T(8,128)(2,1)}, bf16[3,112,768]{2,1,0:T(8,128)(2,1)S(1)}, u32[]{:S(2)}, u32[]{:S(2)}) collective-permute-start(bf16[3,112,768]{2,1,0:T(8,128)(2,1)} %back.5.own), channel_id=1, source_target_pairs={{0,3},{1,2},{2,1},{3,0},{4,5},{5,4},{6,7},{7,6},{8,11},{9,10},{10,... | collective-permute-start | bytes 1548296 | tf_op jit(solution)/shard_map/ppermute | solution.py:201
  209.8 27.1 %all-to-all-start.1 = ((bf16[8,56,1024]{2,1,0:T(8,128)(2,1)}), bf16[8,56,1024]{2,1,0:T(8,128)(2,1)S(1)}, u32[]{:S(2)}, u32[]{:S(2)}) async-start(bf16[8,56,1024]{2,1,0:T(8,128)(2,1)} %bitcast.23), calls=%async_computation.1 | async-start | bytes 1835008 | tf_op jit(solution)/shard_map/all_to_all | solution.py:205
  236.9 19.6 %all-to-all-start.5 = ((bf16[8,56,1024]{2,1,0:T(8,128)(2,1)}), bf16[8,56,1024]{2,1,0:T(8,128)(2,1)}, u32[]{:S(2)}, u32[]{:S(2)}) async-start(bf16[8,56,1024]{2,1,0:T(8,128)(2,1)} %bitcast.22), calls=%async_computation.5 | async-start | bytes 1835008 | tf_op jit(solution)/shard_map/all_to_all | solution.py:205
  243.0 19.1 %collective-permute-start.16 = (bf16[128,1024]{1,0:T(8,128)(2,1)}, bf16[128,1024]{1,0:T(8,128)(2,1)S(1)}, u32[]{:S(2)}, u32[]{:S(2)}) collective-permute-start(bf16[128,1024]{1,0:T(8,128)(2,1)} %get-tuple-element.46), channel_id=1, source_target_pairs={{0,192},{1,193},{2,194},{3,195},{4,196},{5,197},{6,198},{7,199},{8... | collective-permute-start | bytes 786440 | tf_op jit(solution)/shard_map/ppermute | solution.py:194
  245.9 18.5 %collective-permute-start.17 = (bf16[128,1024]{1,0:T(8,128)(2,1)}, bf16[128,1024]{1,0:T(8,128)(2,1)}, u32[]{:S(2)}, u32[]{:S(2)}) collective-permute-start(bf16[128,1024]{1,0:T(8,128)(2,1)} %get-tuple-element.47), channel_id=1, source_target_pairs={{0,64},{1,65},{2,66},{3,67},{4,68},{5,69},{6,70},{7,71},{8,72},{9,... | collective-permute-start | bytes 786440 | tf_op jit(solution)/shard_map/ppermute | solution.py:194
  249.0 30.4 %collective-permute-start.7 = (bf16[128,1024]{1,0:T(8,128)(2,1)}, bf16[128,1024]{1,0:T(8,128)(2,1)S(1)}, u32[]{:S(2)}, u32[]{:S(2)}) collective-permute-start(bf16[128,1024]{1,0:T(8,128)(2,1)} %get-tuple-element.39), channel_id=1, source_target_pairs={{0,224},{1,225},{2,226},{3,227},{4,228},{5,229},{6,230},{7,231},{8... | collective-permute-start | bytes 786440 | tf_op jit(solution)/shard_map/ppermute | solution.py:194
  249.0 30.4 %collective-permute-start.8 = (bf16[128,1024]{1,0:T(8,128)(2,1)}, bf16[128,1024]{1,0:T(8,128)(2,1)S(1)}, u32[]{:S(2)}, u32[]{:S(2)}) collective-permute-start(bf16[128,1024]{1,0:T(8,128)(2,1)} %get-tuple-element.40), channel_id=1, source_target_pairs={{0,32},{1,33},{2,34},{3,35},{4,36},{5,37},{6,38},{7,39},{8,40},{9,... | collective-permute-start | bytes 786440 | tf_op jit(solution)/shard_map/ppermute | solution.py:194
  259.3 26.8 %collective-permute-start.26 = (bf16[128,1024]{1,0:T(8,128)(2,1)S(1)}, bf16[128,1024]{1,0:T(8,128)(2,1)S(1)}, u32[]{:S(2)}, u32[]{:S(2)}) collective-permute-start(bf16[128,1024]{1,0:T(8,128)(2,1)S(1)} %get-tuple-element.53), channel_id=1, source_target_pairs={{0,160},{1,161},{2,162},{3,163},{4,164},{5,165},{6,166},{7,167},{8... | collective-permute-start | bytes 786440 | tf_op jit(solution)/shard_map/ppermute | solution.py:194
  262.1 24.0 %collective-permute-start.27 = (bf16[128,1024]{1,0:T(8,128)(2,1)S(1)}, bf16[128,1024]{1,0:T(8,128)(2,1)S(1)}, u32[]{:S(2)}, u32[]{:S(2)}) collective-permute-start(bf16[128,1024]{1,0:T(8,128)(2,1)S(1)} %get-tuple-element.54), channel_id=1, source_target_pairs={{0,96},{1,97},{2,98},{3,99},{4,100},{5,101},{6,102},{7,103},{8,104... | collective-permute-start | bytes 786440 | tf_op jit(solution)/shard_map/ppermute | solution.py:194
  264.4 31.9 %collective-permute-start.28 = (bf16[128,1024]{1,0:T(8,128)(2,1)S(1)}, bf16[128,1024]{1,0:T(8,128)(2,1)S(1)}, u32[]{:S(2)}, u32[]{:S(2)}) collective-permute-start(bf16[128,1024]{1,0:T(8,128)(2,1)S(1)} %get-tuple-element.55), channel_id=1, source_target_pairs={{0,128},{1,129},{2,130},{3,131},{4,132},{5,133},{6,134},{7,135},{8... | collective-permute-start | bytes 786440 | tf_op jit(solution)/shard_map/ppermute | solution.py:194
  (37 other events, 271.6 us)

commit v2 on v1

--- a/solution.py
+++ b/solution.py
@@ -11,8 +11,36 @@
 F32 = jnp.float32
 GROUP = 8
 META = 16
+COSTS = {'payload': 13284000, 'pick': 35424000, 'partial': 88560000, 'pair': 20664000, 'back': 25092000, 'input_grad': 88560000, 'combine': 18450000, 'fisher': 165312000, 'total': 29520000}
 VMEM = 100 * 1024 * 1024 // 2
 CHUNKS = ((0, -1, 1), (-2, 2), (-3, 3, 4))
+
+ORDER = (
+    ('ring', 2),
+    ('pick', 0),
+    ('ring', 3),
+    ('pick', 1),
+    ('partial', 0),
+    ('ring', 4),
+    ('partial', 1),
+    ('pick', 2),
+    ('pair', 0),
+    ('back', 0),
+    ('pair', 1),
+    ('partial', 2),
+    ('back', 1),
+    ('pair', 2),
+    ('input', 0),
+    ('back', 2),
+    ('input', 1),
+    ('combine', 0),
+    ('input', 2),
+    ('combine', 1),
+    ('total', False),
+    ('combine', 2),
+    ('fisher', 0),
+    ('total', True),
+)
 
 
 def dot(left, right, dims):
@@ -24,9 +52,10 @@
     ins = args[prefetch:]
     in_specs = [whole(a) if s is None else s for a, s in zip(ins, in_specs or [None] * len(ins))]
     out_specs = [whole(a) if s is None else s for a, s in zip(outs, out_specs or [None] * len(outs))]
+    args = list(args[:prefetch]) + list(ins)
     return pl.pallas_call(
         body,
-        out_shape=outs,
+        out_shape=[pltpu.HBM(o.shape, o.dtype) for o in outs],
         grid_spec=pltpu.PrefetchScalarGridSpec(
             num_scalar_prefetch=prefetch,
             grid=grid,
@@ -37,6 +66,7 @@
         compiler_params=pltpu.CompilerParams(
             dimension_semantics=("arbitrary",) * len(grid), vmem_limit_bytes=VMEM
         ),
+        cost_estimate=pl.CostEstimate(flops=COSTS[name] * 300, bytes_accessed=1, transcendentals=0),
         name=name,
     )(*args)
 
@@ -112,28 +142,32 @@
     out[...] = (keep[...].astype(F32) + got[...].astype(F32)).astype(BF)
 
 
+def swiglu_back(gate, up, dact):
+    sig = 1.0 / (1.0 + jnp.exp(-gate))
+    act = gate * sig * up
+    dgate = dact * up * sig * (1.0 + gate * (1.0 - sig))
+    return act.astype(BF), dgate.astype(BF), (dact * gate * sig).astype(BF)
+
+
 def back_body(side, keep, got, more, out):
-    gate, up, dact = (keep[i].astype(F32) + got[i].astype(F32) + more[i].astype(F32) for i in range(3))
-    sig = 1.0 / (1.0 + jnp.exp(-gate))
-    out[0] = (gate * sig * up).astype(BF)
-    out[1] = (dact * up * sig * (1.0 + gate * (1.0 - sig))).astype(BF)
-    out[2] = (dact * gate * sig).astype(BF)
-
-
-def input_body(side, own, near, far, last, gate, up, out, sq, work):
+    sums = (keep[i].astype(F32) + got[i].astype(F32) + more[i].astype(F32) for i in range(3))
+    out[0], out[1], out[2] = swiglu_back(*sums)
+
+
+def places_of(side):
+    h, q = side[0], side[1]
+    return 2 * h + q, 2 * h + 1 - q, 2 * (1 - h) + q, 2 * (1 - h) + 1 - q
+
+
+def input_body(side, own, near, far, last, gate, up, out, work):
     quarter = own.shape[1]
 
     @pl.when(pl.program_id(0) == 0)
     def _():
-        h, q = side[0], side[1]
-        places = (2 * h + q, 2 * h + 1 - q, 2 * (1 - h) + q, 2 * (1 - h) + 1 - q)
-        for place, ref in zip(places, (own, near, far, last)):
+        for place, ref in zip(places_of(side), (own, near, far, last)):
             at = pl.ds(pl.multiple_of(place * quarter, 16), quarter)
-            for i in range(3):
-                v = ref[i].astype(F32)
-                sq[i, at, :] = (v * v).astype(BF)
-                if i:
-                    work[i - 1, at, :] = ref[i]
+            work[0, at, :] = ref[1]
+            work[1, at, :] = ref[2]
 
     out[...] = (dot(work[0], gate[0], ((1,), (1,))) + dot(work[1], up[0], ((1,), (1,)))).astype(BF)
 
@@ -143,21 +177,23 @@
     return (v * v).astype(BF)
 
 
-def fisher_body(scale, *refs):
-    count = (len(refs) - 5) // 2
-    rows, sqs = refs[:count], refs[count : 2 * count]
-    f_gate, f_up, f_down, x_sq, dy_sq = refs[2 * count :]
+def fisher_body(scale, cuts, side, *refs):
+    grads, rows = refs[: sum(cuts)], refs[sum(cuts) : sum(cuts) + len(cuts)]
+    f_gate, f_up, f_down, x_sq, dy_sq = refs[sum(cuts) + len(cuts) :]
     width = x_sq.shape[1]
 
     @pl.when(pl.program_id(0) == 0)
     def _():
         at = 0
-        for ref in rows:
-            x_sq[at : at + ref.shape[0], :] = square_bf(ref[:, :width])
-            dy_sq[at : at + ref.shape[0], :] = square_bf(ref[:, width:])
-            at += ref.shape[0]
-
-    act, dgate, dup = (jnp.concatenate([s[i] for s in sqs], 0) for i in range(3))
+        for ref, cut in zip(rows, cuts):
+            part = ref.shape[0] // cut
+            for place in places_of(side) if cut > 1 else (0,):
+                values = ref[pl.ds(pl.multiple_of(place * part, 16), part), :]
+                x_sq[at : at + part, :] = square_bf(values[:, :width])
+                dy_sq[at : at + part, :] = square_bf(values[:, width:])
+                at += part
+
+    act, dgate, dup = (jnp.concatenate([square_bf(g[i]) for g in grads], 0) for i in range(3))
     f_gate[0] = (dot(x_sq[...], dgate, ((0,), (0,))) * scale).astype(BF)
     f_up[0] = (dot(x_sq[...], dup, ((0,), (0,))) * scale).astype(BF)
     f_down[0] = (dot(act, dy_sq[...], ((0,), (0,))) * scale).astype(BF)
@@ -173,7 +209,7 @@
     total = refs[0][...].astype(F32)
     for ref in refs[1:-1]:
         total = total + ref[...].astype(F32)
-    refs[-1][...] = total.astype(BF)
+    refs[-1][...] = total.astype(refs[-1].dtype)
 
 
 def shape(dims, dtype=BF):
@@ -220,33 +256,52 @@
         [tokens, out_grad, expert_ids.T, route_probs.T],
         "payload",
     )
-    for step in range(1, deep // 2):
-        pays[-step] = along_z(pays[1 - step], 1)
-        pays[step] = along_z(pays[step - 1], -1)
-    pays[deep // 2] = along_z(pays[1 - deep // 2], 1)
+    pays[-1], pays[1] = along_z(pays[0], 1), along_z(pays[0], -1)
 
     tile = 256
     steps = hidden // tile
-    picks, recvs, sqs, parts = [], [], [], []
-    for offsets in CHUNKS:
-        count = len(offsets)
+    last = [pays[0]]
+
+    def run(body, outs, args, name, **kw):
+        at = kw.get("prefetch", 0)
+        args = list(args)
+        args[at], _ = lax.optimization_barrier((args[at], last[0]))
+        outs = call(body, outs, args, name, **kw)
+        last[0] = outs[0]
+        return outs
+
+    made = [{} for _ in CHUNKS]
+
+    def dims(k):
+        count = len(CHUNKS[k])
         per = -(-count * cap // 8) * 8
-        total = GROUP * per
-        half, quarter = total // 2, total // 4
-        send, pick = call(
+        return count, GROUP * per, GROUP * per // 2, GROUP * per // 4
+
+    def ring(step):
+        for sign in (-1, 1):
+            if step < deep // 2 or sign < 0:
+                value, _ = lax.optimization_barrier((pays[sign * (step - 1)], last[0]))
+                pays[sign * step if step < deep // 2 else step] = along_z(value, -sign)
+
+    def pick(k):
+        count, total, _, _ = dims(k)
+        send, made[k]["pick"] = run(
             functools.partial(pick_body, cap),
             [shape((total, 2 * width)), shape((total, count * rows))],
-            [place] + [pays[o] for o in offsets],
+            [place] + [pays[o] for o in CHUNKS[k]],
             "pick",
             prefetch=1,
         )
-        recv = across(send)
+        made[k]["recv"] = across(send)
+
+    def partial(k):
+        _, total, half, _ = dims(k)
         w_in = pl.BlockSpec((1, width, tile), lambda j, s: (0, 0, j))
         half_out = pl.BlockSpec((3, half, tile), lambda j, s: (0, 0, j))
-        give, keep = call(
+        give, made[k]["keep"] = run(
             partial_body,
             [shape((3, half, hidden))] * 2,
-            [side, recv, w_gate, w_up, w_down],
+            [side, made[k]["recv"], w_gate, w_up, w_down],
             "partial",
             grid=(steps,),
             in_specs=[None, w_in, w_in, pl.BlockSpec((1, tile, width), lambda j, s: (0, j, 0))],
@@ -254,56 +309,90 @@
             prefetch=1,
             scratch=[pltpu.VMEM((total, tile), F32)],
         )
-        got = along_x(give, 1)
+        made[k]["got"] = along_x(give, 1)
+
+    def pair(k):
+        quarter = dims(k)[3]
         theirs = pl.BlockSpec((3, quarter, hidden), lambda j, s: (0, 1 - s[1], 0))
+        (give,) = run(
+            pair_body,
+            [shape((3, quarter, hidden))],
+            [side, made[k]["keep"], made[k]["got"]],
+            "pair",
+            in_specs=[theirs, theirs],
+            prefetch=1,
+        )
+        made[k]["more"] = along_x(give, 2)
+
+    def back(k):
+        quarter = dims(k)[3]
         mine = pl.BlockSpec((3, quarter, hidden), lambda j, s: (0, s[1], 0))
-        quarters = shape((3, quarter, hidden))
-        (give,) = call(pair_body, [quarters], [side, keep, got], "pair", in_specs=[theirs, theirs], prefetch=1)
-        more = along_x(give, 2)
-        (own,) = call(
-            back_body, [quarters], [side, keep, got, more], "back", in_specs=[mine, mine, None], prefetch=1
+        (own,) = run(
+            back_body,
+            [shape((3, quarter, hidden))],
+            [side, made[k]["keep"], made[k]["got"], made[k]["more"]],
+            "back",
+            in_specs=[mine, mine, None],
+            prefetch=1,
         )
         near = along_x(own, 2)
-        far = along_x(own, 1)
-        last = along_x(near, 1)
+        made[k]["all"] = [own, near, along_x(own, 1), along_x(near, 1)]
+
+    def input_grad(k):
+        _, total, _, _ = dims(k)
         w_out = pl.BlockSpec((1, tile, hidden), lambda j, s: (0, j, 0))
-        d_rows, sq = call(
+        (d_rows,) = run(
             input_body,
-            [shape((total, width)), shape((3, total, hidden))],
-            [side, own, near, far, last, w_gate, w_up],
+            [shape((total, width))],
+            [side] + made[k]["all"] + [w_gate, w_up],
             "input_grad",
             grid=(width // tile,),
             in_specs=[None] * 4 + [w_out, w_out],
-            out_specs=[pl.BlockSpec((total, tile), lambda j, s: (0, j)), None],
+            out_specs=[pl.BlockSpec((total, tile), lambda j, s: (0, j))],
             prefetch=1,
             scratch=[pltpu.VMEM((2, total, hidden), BF)],
         )
-        back = across(d_rows)
-        sums = call(
+        made[k]["back"] = across(d_rows)
+
+    def combine(k):
+        sums = run(
             combine_body,
-            [shape((rows, width), BF if o else F32) for o in offsets],
-            [pick, back],
+            [shape((rows, width), BF if o else F32) for o in CHUNKS[k]],
+            [made[k]["pick"], made[k]["back"]],
             "combine",
         )
-        for o, s in zip(offsets, sums):
-            parts.append(along_z(s, o) if o else s)
-        recvs.append(recv)
-        sqs.append(sq)
-    (grad_tokens,) = call(total_body, [shape((rows, width))], parts, "total")
-    every = sum(r.shape[0] for r in recvs)
-    f_in = pl.BlockSpec((1, width, tile), lambda j: (0, 0, j))
-    fishers = call(
-        functools.partial(fisher_body, 1.0 / rows),
-        [shape((1, width, hidden)), shape((1, width, hidden)), shape((1, hidden, width))],
-        recvs + sqs,
-        "fisher",
-        grid=(steps,),
-        in_specs=[None] * len(recvs)
-        + [pl.BlockSpec((3, s.shape[1], tile), lambda j: (0, 0, j)) for s in sqs],
-        out_specs=[f_in, f_in, pl.BlockSpec((1, tile, width), lambda j: (0, j, 0))],
-        scratch=[pltpu.VMEM((every, width), BF)] * 2,
-    )
-    return (grad_tokens, *fishers)
+        made[k]["sums"] = [along_z(s, o) if o else s for o, s in zip(CHUNKS[k], sums)]
+
+    def fisher(_):
+        recvs, grads = [m["recv"] for m in made], [g for m in made for g in m["all"]]
+        every = sum(r.shape[0] for r in recvs)
+        f_in = pl.BlockSpec((1, width, tile), lambda j, s: (0, 0, j))
+        fishers.extend(
+            run(
+                functools.partial(fisher_body, 1.0 / rows, [len(m["all"]) for m in made]),
+                [shape((1, width, hidden)), shape((1, width, hidden)), shape((1, hidden, width))],
+                [side] + grads + recvs,
+                "fisher",
+                grid=(steps,),
+                in_specs=[pl.BlockSpec((3, g.shape[1], tile), lambda j, s: (0, 0, j)) for g in grads]
+                + [None] * len(recvs),
+                out_specs=[f_in, f_in, pl.BlockSpec((1, tile, width), lambda j, s: (0, j, 0))],
+                prefetch=1,
+                scratch=[pltpu.VMEM((every, width), BF)] * 2,
+            )
+        )
+
+    def total(last_one):
+        parts = held + [p for m in made for p in m.pop("sums", [])]
+        held[:] = run(total_body, [shape((rows, width), BF if last_one else F32)], parts, "total")
+
+    fishers, held = [], []
+    steps_of = {
+        "pick": pick, "partial": partial, "pair": pair, "back": back, "input": input_grad, "combine": combine, "fisher": fisher, "total": total, "ring": ring,
+    }
+    for step, k in ORDER:
+        steps_of[step](k)
+    return (held[0], *fishers)
 
 
 def solution(mesh):

time: 300 us -> 275 us (0.917)
  waiting for transfers between devices: 142 us -> 113 us
  Pallas kernels: 69.5 us -> 74.5 us
  local copies, waits for them, and re-layouts: 15 us -> 11.4 us
    ppermute x14, waiting for transfers between devices: 70.9 us -> 53.9 us  [along_z(): lax.ppermute(value, ('ep', 'tp'), [(i, (i + step * GROUP * tp) % n) for i...]
    ppermute x15, waiting for transfers between devices: 52.1 us -> 43.8 us  [along_x(): return lax.ppermute(value, ('ep', 'tp'), pairs)]
    pallas_call x21 -> x22, Pallas kernels: 69.5 us -> 74.5 us  [call(): pl.pallas_call(body, out_shape=[pltpu.HBM(o.shape, o.dtype) for o in outs...]
    unnamed x52 -> x68, local copies, waits for them, and re-layouts: 15 us -> 11.4 us
    all_to_all x6, waiting for transfers between devices: 19.3 us -> 15.8 us  [across(): lax.all_to_all(split, 'ep', split_axis=0, concat_axis=0, axis_index_group...]
  transfers between devices with their start and end apart: 35 -> 35, of which waited for: 19 -> 19; matrix products, arithmetic and copies ran while one was open for 0% -> 0% of each run, Pallas kernels for 22% -> 25%
where the time goes in v2:
time: 275 us; the launch traced here: 270 us
  waiting for transfers between devices  113 us (41%)
  Pallas kernels  74.5 us (27%)
  starting transfers between devices  69.9 us (25%)
  local copies, waits for them, and re-layouts  11.4 us (4%)
    pallas_call x22, Pallas kernels, call(): pl.pallas_call(body, out_shape=[pltpu.HBM(o.shape, o.dtype) for o in outs...  74.5 us
    ppermute x14, waiting for transfers between devices, along_z(): lax.ppermute(value, ('ep', 'tp'), [(i, (i + step * GROUP * tp) % n) for i...  53.9 us
    ppermute x15, waiting for transfers between devices, along_x(): return lax.ppermute(value, ('ep', 'tp'), pairs)  43.8 us
    ppermute x14, starting transfers between devices, along_z(): lax.ppermute(value, ('ep', 'tp'), [(i, (i + step * GROUP * tp) % n) for i...  26.4 us
    all_to_all x6, starting transfers between devices, across(): lax.all_to_all(split, 'ep', split_axis=0, concat_axis=0, axis_index_group...  25.7 us
    ppermute x15, starting transfers between devices, along_x(): return lax.ppermute(value, ('ep', 'tp'), pairs)  17.8 us
    all_to_all x6, waiting for transfers between devices, across(): lax.all_to_all(split, 'ep', split_axis=0, concat_axis=0, axis_index_group...  15.8 us
    unnamed x68, local copies, waits for them, and re-layouts  11.4 us
  transfers between devices with their start and end apart: 35, of which 19 were waited for; matrix products, arithmetic and copies ran while one was open for 0% of the time, Pallas kernels for 25%

profile of v2, /device:TPU:64, one launch (start us, length us, event | category | flops | bytes accessed | tf_op | source)
XLA Modules:
  0.0 270.2 jit_solution(5149339929233180771)
XLA Ops:
  6.8 12.7 %collective-permute-done.1.refs_2_ = bf16[272,1024]{1,0:T(8,128)(2,1)S(1)} collective-permute-done((bf16[272,1024]{1,0:T(8,128)(2,1)}, bf16[272,1024]{1,0:T(8,128)(2,1)S(1)}, u32[]{:S(2)}, u32[]{:S(2)}) %collective-permute-start.1) | collective-permute-done | bytes 557088 | tf_op jit(solution)/shard_map/ppermute | solution.py:230
  23.1 4.5 %all-to-all-start.1 = ((bf16[8,56,2048]{2,1,0:T(8,128)(2,1)}), bf16[8,56,2048]{2,1,0:T(8,128)(2,1)S(1)}, u32[]{:S(2)}, u32[]{:S(2)}) async-start(bf16[8,56,2048]{2,1,0:T(8,128)(2,1)} %bitcast.26), calls=%async_computation.1 | async-start | bytes 3670016 | tf_op jit(solution)/shard_map/all_to_all | solution.py:241
  27.6 3.9 %collective-permute-start.3 = (bf16[272,1024]{1,0:T(8,128)(2,1)S(1)}, bf16[272,1024]{1,0:T(8,128)(2,1)}, u32[]{:S(2)}, u32[]{:S(2)}) collective-permute-start(bf16[272,1024]{1,0:T(8,128)(2,1)S(1)} %collective-permute-done.1.refs_2_), channel_id=1, source_target_pairs={{0,224},{1,225},{2,226},{3,227},{4,228},{5,229},{6,230},{7,231},{8... | collective-permute-start | bytes 1671176 | tf_op jit(solution)/shard_map/ppermute | solution.py:230
  31.6 12.5 %collective-permute-done.3.refs_1_ = bf16[272,1024]{1,0:T(8,128)(2,1)} collective-permute-done((bf16[272,1024]{1,0:T(8,128)(2,1)S(1)}, bf16[272,1024]{1,0:T(8,128)(2,1)}, u32[]{:S(2)}, u32[]{:S(2)}) %collective-permute-start.3) | collective-permute-done | bytes 557088 | tf_op jit(solution)/shard_map/ppermute | solution.py:230
  53.7 4.4 %all-to-all-start = ((bf16[8,40,2048]{2,1,0:T(8,128)(2,1)}), bf16[8,40,2048]{2,1,0:T(8,128)(2,1)S(1)}, u32[]{:S(2)}, u32[]{:S(2)}) async-start(bf16[8,40,2048]{2,1,0:T(8,128)(2,1)} %bitcast.28), calls=%async_computation | async-start | bytes 2621440 | tf_op jit(solution)/shard_map/all_to_all | solution.py:241
  59.6 6.3 %partial.3 = (bf16[3,224,768]{2,1,0:T(8,128)(2,1)}, bf16[3,224,768]{2,1,0:T(8,128)(2,1)}) custom-call(s32[2]{0:T(128)S(1)} %pad_add_fusion.side, bf16[448,2048]{1,0:T(8,128)(2,1)} %bitcast.24, bf16[1,1024,768]{2,1,0:T(8,128)(2,1)S(1)} %copy-done.1, bf16[1,1024,768]{2,1,0:T(8,128)(2,1)S(1)} %copy-done.2, bf16[1,768,1024]{2,1,0:T(8,128)(2,1)} %down.5), custom_call_target="tpu_custom_call" | custom-call | flops 26567999488 | bytes 1 | tf_op jit(solution)/shard_map/partial/pallas_call | solution.py:56
  69.2 7.8 %all-to-all-done = bf16[8,40,2048]{2,1,0:T(8,128)(2,1)S(1)} async-done(((bf16[8,40,2048]{2,1,0:T(8,128)(2,1)}), bf16[8,40,2048]{2,1,0:T(8,128)(2,1)S(1)}, u32[]{:S(2)}, u32[]{:S(2)}) %all-to-all-start) | async-done | bytes 1310752 | tf_op jit(solution)/shard_map/all_to_all | solution.py:241
  77.0 5.4 %partial.4 = (bf16[3,160,768]{2,1,0:T(8,128)(2,1)}, bf16[3,160,768]{2,1,0:T(8,128)(2,1)}) custom-call(s32[2]{0:T(128)S(1)} %pad_add_fusion.side, bf16[320,2048]{1,0:T(8,128)(2,1)S(1)} %bitcast.17, bf16[1,1024,768]{2,1,0:T(8,128)(2,1)S(1)} %copy-done.1, bf16[1,1024,768]{2,1,0:T(8,128)(2,1)} %up.11, bf16[1,768,1024]{2,1,0:T(8,128)(2,1)} %down.5), custom_call_target="tpu_custom_call" | custom-call | flops 26567999488 | bytes 1 | tf_op jit(solution)/shard_map/partial/pallas_call | solution.py:56
  91.6 4.5 %all-to-all-start.2 = ((bf16[8,56,2048]{2,1,0:T(8,128)(2,1)}), bf16[8,56,2048]{2,1,0:T(8,128)(2,1)}, u32[]{:S(2)}, u32[]{:S(2)}) async-start(bf16[8,56,2048]{2,1,0:T(8,128)(2,1)} %bitcast.27), calls=%async_computation.2 | async-start | bytes 3670016 | tf_op jit(solution)/shard_map/all_to_all | solution.py:241
  104.9 7.3 %collective-permute-done.9.got = bf16[3,160,768]{2,1,0:T(8,128)(2,1)S(1)} collective-permute-done((bf16[3,160,768]{2,1,0:T(8,128)(2,1)}, bf16[3,160,768]{2,1,0:T(8,128)(2,1)S(1)}, u32[]{:S(2)}, u32[]{:S(2)}) %collective-permute-start.9) | collective-permute-done | bytes 737312 | tf_op jit(solution)/shard_map/ppermute | solution.py:237
  115.3 5.1 %all-to-all-done.2 = bf16[8,56,2048]{2,1,0:T(8,128)(2,1)} async-done(((bf16[8,56,2048]{2,1,0:T(8,128)(2,1)}), bf16[8,56,2048]{2,1,0:T(8,128)(2,1)}, u32[]{:S(2)}, u32[]{:S(2)}) %all-to-all-start.2) | async-done | bytes 1835040 | tf_op jit(solution)/shard_map/all_to_all | solution.py:241
  120.4 6.3 %partial.5 = (bf16[3,224,768]{2,1,0:T(8,128)(2,1)}, bf16[3,224,768]{2,1,0:T(8,128)(2,1)}) custom-call(s32[2]{0:T(128)S(1)} %pad_add_fusion.side, bf16[448,2048]{1,0:T(8,128)(2,1)} %bitcast.10.rows_ref.refs_14_, bf16[1,1024,768]{2,1,0:T(8,128)(2,1)S(1)} %copy-done.1, bf16[1,1024,768]{2,1,0:T(8,128)(2,1)S(1)} %copy-done.3, bf16[1,768,1024]{2,1,0:T(8,128)(2,1)} %down.5), custom_call_target="tpu_custom_call" | custom-call | flops 26567999488 | bytes 1 | tf_op jit(solution)/shard_map/partial/pallas_call | solution.py:56
  133.6 8.1 %collective-permute-done.16.near.refs_5_ = bf16[3,80,768]{2,1,0:T(8,128)(2,1)} collective-permute-done((bf16[3,80,768]{2,1,0:T(8,128)(2,1)}, bf16[3,80,768]{2,1,0:T(8,128)(2,1)}, u32[]{:S(2)}, u32[]{:S(2)}) %collective-permute-start.16) | collective-permute-done | bytes 368672 | tf_op jit(solution)/shard_map/ppermute | solution.py:237
  152.6 9.6 %collective-permute-done.14.last.refs_3_ = bf16[3,112,768]{2,1,0:T(8,128)(2,1)S(1)} collective-permute-done((bf16[3,112,768]{2,1,0:T(8,128)(2,1)}, bf16[3,112,768]{2,1,0:T(8,128)(2,1)S(1)}, u32[]{:S(2)}, u32[]{:S(2)}) %collective-permute-start.14) | collective-permute-done | bytes 516128 | tf_op jit(solution)/shard_map/ppermute | solution.py:237
  162.2 5.3 %input_grad.3 = bf16[448,1024]{1,0:T(8,128)(2,1)} custom-call(s32[2]{0:T(128)S(1)} %pad_add_fusion.side, bf16[3,112,768]{2,1,0:T(8,128)(2,1)S(1)} %copy-done.9, bf16[3,112,768]{2,1,0:T(8,128)(2,1)} %collective-permute-done.12.near.refs_1_, bf16[3,112,768]{2,1,0:T(8,128)(2,1)S(1)} %collective-permute-done.13.far.refs_2_, ...), custom_call_target="tpu_custom_call" | custom-call | flops 26567999488 | bytes 1 | tf_op jit(solution)/shard_map/input_grad/pallas_call | solution.py:56
  177.2 5.2 %input_grad.4 = bf16[320,1024]{1,0:T(8,128)(2,1)} custom-call(s32[2]{0:T(128)S(1)} %pad_add_fusion.side, bf16[3,80,768]{2,1,0:T(8,128)(2,1)S(1)} %copy-done.17, bf16[3,80,768]{2,1,0:T(8,128)(2,1)} %collective-permute-done.16.near.refs_5_, bf16[3,80,768]{2,1,0:T(8,128)(2,1)} %collective-permute-done.17.far.refs_6_, ...), custom_call_target="tpu_custom_call" | custom-call | flops 26567999488 | bytes 1 | tf_op jit(solution)/shard_map/input_grad/pallas_call | solution.py:56
  182.4 8.4 %collective-permute-done.19.near.refs_9_ = bf16[3,112,768]{2,1,0:T(8,128)(2,1)} collective-permute-done((bf16[3,112,768]{2,1,0:T(8,128)(2,1)}, bf16[3,112,768]{2,1,0:T(8,128)(2,1)}, u32[]{:S(2)}, u32[]{:S(2)}) %collective-permute-start.19) | collective-permute-done | bytes 516128 | tf_op jit(solution)/shard_map/ppermute | solution.py:237
  190.9 5.2 %all-to-all-start.4 = ((bf16[8,40,1024]{2,1,0:T(8,128)(2,1)}), bf16[8,40,1024]{2,1,0:T(8,128)(2,1)S(1)}, u32[]{:S(2)}, u32[]{:S(2)}) async-start(bf16[8,40,1024]{2,1,0:T(8,128)(2,1)} %bitcast.31), calls=%async_computation.4 | async-start | bytes 1310720 | tf_op jit(solution)/shard_map/all_to_all | solution.py:241
  201.3 5.7 %input_grad.5 = bf16[448,1024]{1,0:T(8,128)(2,1)} custom-call(s32[2]{0:T(128)S(1)} %pad_add_fusion.side, bf16[3,112,768]{2,1,0:T(8,128)(2,1)S(1)} %copy-done.15, bf16[3,112,768]{2,1,0:T(8,128)(2,1)} %collective-permute-done.19.near.refs_9_, bf16[3,112,768]{2,1,0:T(8,128)(2,1)} %collective-permute-done.20.far.refs_10_, ...), custom_call_target="tpu_custom_call" | custom-call | flops 26567999488 | bytes 1 | tf_op jit(solution)/shard_map/input_grad/pallas_call | solution.py:56
  210.0 4.4 %collective-permute-start.25 = (bf16[128,1024]{1,0:T(8,128)(2,1)}, bf16[128,1024]{1,0:T(8,128)(2,1)S(1)}, u32[]{:S(2)}, u32[]{:S(2)}) collective-permute-start(bf16[128,1024]{1,0:T(8,128)(2,1)} %get-tuple-element.89), channel_id=1, source_target_pairs={{0,64},{1,65},{2,66},{3,67},{4,68},{5,69},{6,70},{7,71},{8,72},{9,... | collective-permute-start | bytes 786440 | tf_op jit(solution)/shard_map/ppermute | solution.py:230
  218.8 8.4 %collective-permute-done.25.refs_4_ = bf16[128,1024]{1,0:T(8,128)(2,1)S(1)} collective-permute-done((bf16[128,1024]{1,0:T(8,128)(2,1)}, bf16[128,1024]{1,0:T(8,128)(2,1)S(1)}, u32[]{:S(2)}, u32[]{:S(2)}) %collective-permute-start.25) | collective-permute-done | bytes 262176 | tf_op jit(solution)/shard_map/ppermute | solution.py:230
  243.2 12.1 %fisher.1 = (bf16[1,1024,768]{2,1,0:T(8,128)(2,1)}, bf16[1,1024,768]{2,1,0:T(8,128)(2,1)}, bf16[1,768,1024]{2,1,0:T(8,128)(2,1)}) custom-call(s32[2]{0:T(128)S(1)} %pad_add_fusion.side, bf16[3,112,768]{2,1,0:T(8,128)(2,1)S(1)} %copy-done.10, bf16[3,112,768]{2,1,0:T(8,128)(2,1)} %collective-permute-done.12.near.refs_1_, bf16[3,112,768]{2,1,0:T(8,128)(2,1)S(1)} %copy-done.12, ...), custom_call_target="tpu_custom_call" | custom-call | flops 49593597952 | bytes 1 | tf_op jit(solution)/shard_map/fisher/pallas_call | solution.py:56
  255.3 6.7 %collective-permute-done.27.refs_2_ = bf16[128,1024]{1,0:T(8,128)(2,1)S(1)} collective-permute-done((bf16[128,1024]{1,0:T(8,128)(2,1)}, bf16[128,1024]{1,0:T(8,128)(2,1)S(1)}, u32[]{:S(2)}, u32[]{:S(2)}) %collective-permute-start.27) | collective-permute-done | bytes 262176 | tf_op jit(solution)/shard_map/ppermute | solution.py:230
  261.9 7.5 %collective-permute-done.28.refs_3_ = bf16[128,1024]{1,0:T(8,128)(2,1)S(1)} collective-permute-done((bf16[128,1024]{1,0:T(8,128)(2,1)}, bf16[128,1024]{1,0:T(8,128)(2,1)S(1)}, u32[]{:S(2)}, u32[]{:S(2)}) %collective-permute-start.28) | collective-permute-done | bytes 262176 | tf_op jit(solution)/shard_map/ppermute | solution.py:230
  (137 shorter events, 102.0 us)
Async XLA Ops:
  23.1 29.4 %all-to-all-start.1 = ((bf16[8,56,2048]{2,1,0:T(8,128)(2,1)}), bf16[8,56,2048]{2,1,0:T(8,128)(2,1)S(1)}, u32[]{:S(2)}, u32[]{:S(2)}) async-start(bf16[8,56,2048]{2,1,0:T(8,128)(2,1)} %bitcast.26), calls=%async_computation.1 | async-start | bytes 3670016 | tf_op jit(solution)/shard_map/all_to_all | solution.py:241
  27.6 16.5 %collective-permute-start.3 = (bf16[272,1024]{1,0:T(8,128)(2,1)S(1)}, bf16[272,1024]{1,0:T(8,128)(2,1)}, u32[]{:S(2)}, u32[]{:S(2)}) collective-permute-start(bf16[272,1024]{1,0:T(8,128)(2,1)S(1)} %collective-permute-done.1.refs_2_), channel_id=1, source_target_pairs={{0,224},{1,225},{2,226},{3,227},{4,228},{5,229},{6,230},{7,231},{8... | collective-permute-start | bytes 1671176 | tf_op jit(solution)/shard_map/ppermute | solution.py:230
  47.5 19.9 %collective-permute-start.4 = (bf16[272,1024]{1,0:T(8,128)(2,1)}, bf16[272,1024]{1,0:T(8,128)(2,1)}, u32[]{:S(2)}, u32[]{:S(2)}) collective-permute-start(bf16[272,1024]{1,0:T(8,128)(2,1)} %collective-permute-done.2.refs_0_), channel_id=1, source_target_pairs={{0,32},{1,33},{2,34},{3,35},{4,36},{5,37},{6,38},{7,39},{8,40},{9,... | collective-permute-start | bytes 1671176 | tf_op jit(solution)/shard_map/ppermute | solution.py:230
  47.5 34.9 %collective-permute-start.5 = (bf16[272,1024]{1,0:T(8,128)(2,1)}, bf16[272,1024]{1,0:T(8,128)(2,1)}, u32[]{:S(2)}, u32[]{:S(2)}) collective-permute-start(bf16[272,1024]{1,0:T(8,128)(2,1)} %collective-permute-done.3.refs_1_), channel_id=1, source_target_pairs={{0,224},{1,225},{2,226},{3,227},{4,228},{5,229},{6,230},{7,231},{8... | collective-permute-start | bytes 1671176 | tf_op jit(solution)/shard_map/ppermute | solution.py:230
  53.7 23.2 %all-to-all-start = ((bf16[8,40,2048]{2,1,0:T(8,128)(2,1)}), bf16[8,40,2048]{2,1,0:T(8,128)(2,1)S(1)}, u32[]{:S(2)}, u32[]{:S(2)}) async-start(bf16[8,40,2048]{2,1,0:T(8,128)(2,1)} %bitcast.28), calls=%async_computation | async-start | bytes 2621440 | tf_op jit(solution)/shard_map/all_to_all | solution.py:241
  65.9 20.8 %collective-permute-start.7 = (bf16[3,224,768]{2,1,0:T(8,128)(2,1)}, bf16[3,224,768]{2,1,0:T(8,128)(2,1)}, u32[]{:S(2)}, u32[]{:S(2)}) collective-permute-start(bf16[3,224,768]{2,1,0:T(8,128)(2,1)} %get-tuple-element.60), channel_id=1, source_target_pairs={{0,1},{1,0},{2,3},{3,2},{4,7},{5,6},{6,5},{7,4},{8,9},{9,8},{10,11... | collective-permute-start | bytes 3096584 | tf_op jit(solution)/shard_map/ppermute | solution.py:237
  91.6 28.9 %all-to-all-start.2 = ((bf16[8,56,2048]{2,1,0:T(8,128)(2,1)}), bf16[8,56,2048]{2,1,0:T(8,128)(2,1)}, u32[]{:S(2)}, u32[]{:S(2)}) async-start(bf16[8,56,2048]{2,1,0:T(8,128)(2,1)} %bitcast.27), calls=%async_computation.2 | async-start | bytes 3670016 | tf_op jit(solution)/shard_map/all_to_all | solution.py:241
  102.6 29.0 %collective-permute-start.12 = (bf16[3,112,768]{2,1,0:T(8,128)(2,1)}, bf16[3,112,768]{2,1,0:T(8,128)(2,1)}, u32[]{:S(2)}, u32[]{:S(2)}) collective-permute-start(bf16[3,112,768]{2,1,0:T(8,128)(2,1)} %back.3.own.refs_0_), channel_id=1, source_target_pairs={{0,3},{1,2},{2,1},{3,0},{4,5},{5,4},{6,7},{7,6},{8,11},{9,10},{10,... | collective-permute-start | bytes 1548296 | tf_op jit(solution)/shard_map/ppermute | solution.py:237
  126.8 18.8 %collective-permute-start.11 = (bf16[3,224,768]{2,1,0:T(8,128)(2,1)}, bf16[3,224,768]{2,1,0:T(8,128)(2,1)S(1)}, u32[]{:S(2)}, u32[]{:S(2)}) collective-permute-start(bf16[3,224,768]{2,1,0:T(8,128)(2,1)} %get-tuple-element.73), channel_id=1, source_target_pairs={{0,1},{1,0},{2,3},{3,2},{4,7},{5,6},{6,5},{7,4},{8,9},{9,8},{10,11... | collective-permute-start | bytes 3096584 | tf_op jit(solution)/shard_map/ppermute | solution.py:237
  130.3 22.3 %collective-permute-start.13 = (bf16[3,112,768]{2,1,0:T(8,128)(2,1)S(1)}, bf16[3,112,768]{2,1,0:T(8,128)(2,1)S(1)}, u32[]{:S(2)}, u32[]{:S(2)}) collective-permute-start(bf16[3,112,768]{2,1,0:T(8,128)(2,1)S(1)} %copy-done.9), channel_id=1, source_target_pairs={{0,1},{1,0},{2,3},{3,2},{4,7},{5,6},{6,5},{7,4},{8,9},{9,8},{10,11... | collective-permute-start | bytes 1548296 | tf_op jit(solution)/shard_map/ppermute | solution.py:237
  131.6 30.6 %collective-permute-start.14 = (bf16[3,112,768]{2,1,0:T(8,128)(2,1)}, bf16[3,112,768]{2,1,0:T(8,128)(2,1)S(1)}, u32[]{:S(2)}, u32[]{:S(2)}) collective-permute-start(bf16[3,112,768]{2,1,0:T(8,128)(2,1)} %collective-permute-done.12.near.refs_1_), channel_id=1, source_target_pairs={{0,1},{1,0},{2,3},{3,2},{4,7},{5,6},{6,5},{7,4},{8,9},{9,8},{10,11... | collective-permute-start | bytes 1548296 | tf_op jit(solution)/shard_map/ppermute | solution.py:237
  132.3 44.8 %collective-permute-start.17 = (bf16[3,80,768]{2,1,0:T(8,128)(2,1)}, bf16[3,80,768]{2,1,0:T(8,128)(2,1)}, u32[]{:S(2)}, u32[]{:S(2)}) collective-permute-start(bf16[3,80,768]{2,1,0:T(8,128)(2,1)} %back.4.own.refs_4_), channel_id=1, source_target_pairs={{0,1},{1,0},{2,3},{3,2},{4,7},{5,6},{6,5},{7,4},{8,9},{9,8},{10,11... | collective-permute-start | bytes 1105928 | tf_op jit(solution)/shard_map/ppermute | solution.py:237
  141.7 35.5 %collective-permute-start.18 = (bf16[3,80,768]{2,1,0:T(8,128)(2,1)}, bf16[3,80,768]{2,1,0:T(8,128)(2,1)}, u32[]{:S(2)}, u32[]{:S(2)}) collective-permute-start(bf16[3,80,768]{2,1,0:T(8,128)(2,1)} %collective-permute-done.16.near.refs_5_), channel_id=1, source_target_pairs={{0,1},{1,0},{2,3},{3,2},{4,7},{5,6},{6,5},{7,4},{8,9},{9,8},{10,11... | collective-permute-start | bytes 1105928 | tf_op jit(solution)/shard_map/ppermute | solution.py:237
  147.1 24.0 %collective-permute-start.15 = (bf16[3,112,768]{2,1,0:T(8,128)(2,1)}, bf16[3,112,768]{2,1,0:T(8,128)(2,1)S(1)}, u32[]{:S(2)}, u32[]{:S(2)}) collective-permute-start(bf16[3,112,768]{2,1,0:T(8,128)(2,1)} %pair.5), channel_id=1, source_target_pairs={{0,3},{1,2},{2,1},{3,0},{4,5},{5,4},{6,7},{7,6},{8,11},{9,10},{10,... | collective-permute-start | bytes 1548296 | tf_op jit(solution)/shard_map/ppermute | solution.py:237
  167.5 23.3 %all-to-all-start.3 = ((bf16[8,56,1024]{2,1,0:T(8,128)(2,1)}), bf16[8,56,1024]{2,1,0:T(8,128)(2,1)S(1)}, u32[]{:S(2)}, u32[]{:S(2)}) async-start(bf16[8,56,1024]{2,1,0:T(8,128)(2,1)} %bitcast.30), calls=%async_computation.3 | async-start | bytes 1835008 | tf_op jit(solution)/shard_map/all_to_all | solution.py:241
  175.3 26.0 %collective-permute-start.20 = (bf16[3,112,768]{2,1,0:T(8,128)(2,1)}, bf16[3,112,768]{2,1,0:T(8,128)(2,1)}, u32[]{:S(2)}, u32[]{:S(2)}) collective-permute-start(bf16[3,112,768]{2,1,0:T(8,128)(2,1)} %back.5.own.refs_8_), channel_id=1, source_target_pairs={{0,1},{1,0},{2,3},{3,2},{4,7},{5,6},{6,5},{7,4},{8,9},{9,8},{10,11... | collective-permute-start | bytes 1548296 | tf_op jit(solution)/shard_map/ppermute | solution.py:237
  190.9 17.0 %all-to-all-start.4 = ((bf16[8,40,1024]{2,1,0:T(8,128)(2,1)}), bf16[8,40,1024]{2,1,0:T(8,128)(2,1)S(1)}, u32[]{:S(2)}, u32[]{:S(2)}) async-start(bf16[8,40,1024]{2,1,0:T(8,128)(2,1)} %bitcast.31), calls=%async_computation.4 | async-start | bytes 1310720 | tf_op jit(solution)/shard_map/all_to_all | solution.py:241
  198.4 20.3 %collective-permute-start.22 = (bf16[128,1024]{1,0:T(8,128)(2,1)}, bf16[128,1024]{1,0:T(8,128)(2,1)S(1)}, u32[]{:S(2)}, u32[]{:S(2)}) collective-permute-start(bf16[128,1024]{1,0:T(8,128)(2,1)} %get-tuple-element.87), channel_id=1, source_target_pairs={{0,224},{1,225},{2,226},{3,227},{4,228},{5,229},{6,230},{7,231},{8... | collective-permute-start | bytes 786440 | tf_op jit(solution)/shard_map/ppermute | solution.py:230
  201.3 17.4 %collective-permute-start.23 = (bf16[128,1024]{1,0:T(8,128)(2,1)}, bf16[128,1024]{1,0:T(8,128)(2,1)}, u32[]{:S(2)}, u32[]{:S(2)}) collective-permute-start(bf16[128,1024]{1,0:T(8,128)(2,1)} %get-tuple-element.88), channel_id=1, source_target_pairs={{0,32},{1,33},{2,34},{3,35},{4,36},{5,37},{6,38},{7,39},{8,40},{9,... | collective-permute-start | bytes 786440 | tf_op jit(solution)/shard_map/ppermute | solution.py:230
  210.0 17.2 %collective-permute-start.25 = (bf16[128,1024]{1,0:T(8,128)(2,1)}, bf16[128,1024]{1,0:T(8,128)(2,1)S(1)}, u32[]{:S(2)}, u32[]{:S(2)}) collective-permute-start(bf16[128,1024]{1,0:T(8,128)(2,1)} %get-tuple-element.89), channel_id=1, source_target_pairs={{0,64},{1,65},{2,66},{3,67},{4,68},{5,69},{6,70},{7,71},{8,72},{9,... | collective-permute-start | bytes 786440 | tf_op jit(solution)/shard_map/ppermute | solution.py:230
  215.2 18.0 %all-to-all-start.5 = ((bf16[8,56,1024]{2,1,0:T(8,128)(2,1)}), bf16[8,56,1024]{2,1,0:T(8,128)(2,1)S(1)}, u32[]{:S(2)}, u32[]{:S(2)}) async-start(bf16[8,56,1024]{2,1,0:T(8,128)(2,1)} %bitcast.29), calls=%async_computation.5 | async-start | bytes 1835008 | tf_op jit(solution)/shard_map/all_to_all | solution.py:241
  234.5 34.9 %collective-permute-start.26 = (bf16[128,1024]{1,0:T(8,128)(2,1)}, bf16[128,1024]{1,0:T(8,128)(2,1)S(1)}, u32[]{:S(2)}, u32[]{:S(2)}) collective-permute-start(bf16[128,1024]{1,0:T(8,128)(2,1)} %get-tuple-element.92), channel_id=1, source_target_pairs={{0,160},{1,161},{2,162},{3,163},{4,164},{5,165},{6,166},{7,167},{8... | collective-permute-start | bytes 786440 | tf_op jit(solution)/shard_map/ppermute | solution.py:230
  237.9 24.0 %collective-permute-start.27 = (bf16[128,1024]{1,0:T(8,128)(2,1)}, bf16[128,1024]{1,0:T(8,128)(2,1)S(1)}, u32[]{:S(2)}, u32[]{:S(2)}) collective-permute-start(bf16[128,1024]{1,0:T(8,128)(2,1)} %get-tuple-element.96), channel_id=1, source_target_pairs={{0,96},{1,97},{2,98},{3,99},{4,100},{5,101},{6,102},{7,103},{8,104... | collective-permute-start | bytes 786440 | tf_op jit(solution)/shard_map/ppermute | solution.py:230
  239.6 29.8 %collective-permute-start.28 = (bf16[128,1024]{1,0:T(8,128)(2,1)}, bf16[128,1024]{1,0:T(8,128)(2,1)S(1)}, u32[]{:S(2)}, u32[]{:S(2)}) collective-permute-start(bf16[128,1024]{1,0:T(8,128)(2,1)} %get-tuple-element.97), channel_id=1, source_target_pairs={{0,128},{1,129},{2,130},{3,131},{4,132},{5,133},{6,134},{7,135},{8... | collective-permute-start | bytes 786440 | tf_op jit(solution)/shard_map/ppermute | solution.py:230
  (45 other events, 391.7 us)

commit v3 on v2

--- a/solution.py
+++ b/solution.py
@@ -11,34 +11,34 @@
 F32 = jnp.float32
 GROUP = 8
 META = 16
-COSTS = {'payload': 13284000, 'pick': 35424000, 'partial': 88560000, 'pair': 20664000, 'back': 25092000, 'input_grad': 88560000, 'combine': 18450000, 'fisher': 165312000, 'total': 29520000}
+COSTS = {'payload': 33210000, 'pick': 88560000, 'partial': 22140000, 'pair': 51660000, 'back': 62730000, 'input_grad': 221400000, 'combine': 46125000, 'fisher': 413280000, 'total': 73800000}
 VMEM = 100 * 1024 * 1024 // 2
-CHUNKS = ((0, -1, 1), (-2, 2), (-3, 3, 4))
+CHUNKS = ([0, -1, 1], [-2, 2], [-3, 3, 4])
 
 ORDER = (
     ('ring', 2),
+    ('ring', 3),
+    ('ring', 4),
     ('pick', 0),
-    ('ring', 3),
     ('pick', 1),
     ('partial', 0),
-    ('ring', 4),
     ('partial', 1),
     ('pick', 2),
     ('pair', 0),
+    ('pair', 1),
     ('back', 0),
-    ('pair', 1),
     ('partial', 2),
+    ('input', 0),
     ('back', 1),
     ('pair', 2),
-    ('input', 0),
     ('back', 2),
+    ('combine', 0),
     ('input', 1),
-    ('combine', 0),
     ('input', 2),
     ('combine', 1),
-    ('total', False),
     ('combine', 2),
     ('fisher', 0),
+    ('total', False),
     ('total', True),
 )
 

time: 275 us -> 270 us (0.982); the launches traced: 270 us -> 268 us
  waiting for transfers between devices: 113 us -> 109 us
    all_to_all x6, waiting for transfers between devices: 15.8 us -> 41 us  [across(): lax.all_to_all(split, 'ep', split_axis=0, concat_axis=0, axis_index_group...]
    ppermute x14, waiting for transfers between devices: 53.9 us -> 34.6 us  [along_z(): lax.ppermute(value, ('ep', 'tp'), [(i, (i + step * GROUP * tp) % n) for i...]
    ppermute x15, waiting for transfers between devices: 43.8 us -> 33 us  [along_x(): return lax.ppermute(value, ('ep', 'tp'), pairs)]
    unnamed x68 -> x60, local copies, waits for them, and re-layouts: 11.4 us -> 12.3 us
  transfers between devices with their start and end apart: 35 -> 35, of which waited for: 19 -> 14; matrix products, arithmetic and copies ran while one was open for 0% -> 0% of each run, Pallas kernels for 25% -> 26%
where the time goes in v3:
time: 270 us; the launch traced here: 268 us
  waiting for transfers between devices  109 us (40%)
  Pallas kernels  74.8 us (28%)
  starting transfers between devices  71.4 us (26%)
  local copies, waits for them, and re-layouts  12.3 us (5%)
    pallas_call x22, Pallas kernels, call(): pl.pallas_call(body, out_shape=[pltpu.HBM(o.shape, o.dtype) for o in outs...  74.8 us
    all_to_all x6, waiting for transfers between devices, across(): lax.all_to_all(split, 'ep', split_axis=0, concat_axis=0, axis_index_group...  41 us
    ppermute x14, waiting for transfers between devices, along_z(): lax.ppermute(value, ('ep', 'tp'), [(i, (i + step * GROUP * tp) % n) for i...  34.6 us
    ppermute x15, waiting for transfers between devices, along_x(): return lax.ppermute(value, ('ep', 'tp'), pairs)  33 us
    ppermute x14, starting transfers between devices, along_z(): lax.ppermute(value, ('ep', 'tp'), [(i, (i + step * GROUP * tp) % n) for i...  26.8 us
    all_to_all x6, starting transfers between devices, across(): lax.all_to_all(split, 'ep', split_axis=0, concat_axis=0, axis_index_group...  26.1 us
    ppermute x15, starting transfers between devices, along_x(): return lax.ppermute(value, ('ep', 'tp'), pairs)  18.4 us
    unnamed x60, local copies, waits for them, and re-layouts  12.3 us
  transfers between devices with their start and end apart: 35, of which 14 were waited for; matrix products, arithmetic and copies ran while one was open for 0% of the time, Pallas kernels for 26%

profile of v3, /device:TPU:64, one launch (start us, length us, event | category | flops | bytes accessed | tf_op | source)
XLA Modules:
  0.0 268.1 jit_solution(14195000828449078943)
XLA Ops:
  6.8 12.7 %collective-permute-done.1.refs_2_ = bf16[272,1024]{1,0:T(8,128)(2,1)S(1)} collective-permute-done((bf16[272,1024]{1,0:T(8,128)(2,1)}, bf16[272,1024]{1,0:T(8,128)(2,1)S(1)}, u32[]{:S(2)}, u32[]{:S(2)}) %collective-permute-start.1) | collective-permute-done | bytes 557088 | tf_op jit(solution)/shard_map/ppermute | solution.py:230
  26.3 4.5 %all-to-all-start.1 = ((bf16[8,56,2048]{2,1,0:T(8,128)(2,1)}), bf16[8,56,2048]{2,1,0:T(8,128)(2,1)}, u32[]{:S(2)}, u32[]{:S(2)}) async-start(bf16[8,56,2048]{2,1,0:T(8,128)(2,1)} %bitcast.25), calls=%async_computation.1 | async-start | bytes 3670016 | tf_op jit(solution)/shard_map/all_to_all | solution.py:241
  30.7 4.5 %collective-permute-done.2.refs_0_ = bf16[272,1024]{1,0:T(8,128)(2,1)} collective-permute-done((bf16[272,1024]{1,0:T(8,128)(2,1)S(1)}, bf16[272,1024]{1,0:T(8,128)(2,1)}, u32[]{:S(2)}, u32[]{:S(2)}) %collective-permute-start.2) | collective-permute-done | bytes 557088 | tf_op jit(solution)/shard_map/ppermute | solution.py:230
  39.6 15.6 %all-to-all-done.1 = bf16[8,56,2048]{2,1,0:T(8,128)(2,1)} async-done(((bf16[8,56,2048]{2,1,0:T(8,128)(2,1)}), bf16[8,56,2048]{2,1,0:T(8,128)(2,1)}, u32[]{:S(2)}, u32[]{:S(2)}) %all-to-all-start.1) | async-done | bytes 1835040 | tf_op jit(solution)/shard_map/all_to_all | solution.py:241
  63.7 6.3 %partial.3 = (bf16[3,224,768]{2,1,0:T(8,128)(2,1)}, bf16[3,224,768]{2,1,0:T(8,128)(2,1)}) custom-call(s32[2]{0:T(128)S(1)} %pad_add_fusion.side, bf16[448,2048]{1,0:T(8,128)(2,1)} %bitcast.8.rows_ref.refs_12_, bf16[1,1024,768]{2,1,0:T(8,128)(2,1)S(1)} %copy-done.1, bf16[1,1024,768]{2,1,0:T(8,128)(2,1)S(1)} %copy-done.2, bf16[1,768,1024]{2,1,0:T(8,128)(2,1)} %down.5), custom_call_target="tpu_custom_call" | custom-call | flops 6641999872 | bytes 1 | tf_op jit(solution)/shard_map/partial/pallas_call | solution.py:56
  71.5 6.0 %all-to-all-done = bf16[8,40,2048]{2,1,0:T(8,128)(2,1)S(1)} async-done(((bf16[8,40,2048]{2,1,0:T(8,128)(2,1)}), bf16[8,40,2048]{2,1,0:T(8,128)(2,1)S(1)}, u32[]{:S(2)}, u32[]{:S(2)}) %all-to-all-start) | async-done | bytes 1310752 | tf_op jit(solution)/shard_map/all_to_all | solution.py:241
  77.5 5.5 %partial.4 = (bf16[3,160,768]{2,1,0:T(8,128)(2,1)}, bf16[3,160,768]{2,1,0:T(8,128)(2,1)}) custom-call(s32[2]{0:T(128)S(1)} %pad_add_fusion.side, bf16[320,2048]{1,0:T(8,128)(2,1)S(1)} %bitcast.17, bf16[1,1024,768]{2,1,0:T(8,128)(2,1)S(1)} %copy-done.1, bf16[1,1024,768]{2,1,0:T(8,128)(2,1)} %up.11, bf16[1,768,1024]{2,1,0:T(8,128)(2,1)} %down.5), custom_call_target="tpu_custom_call" | custom-call | flops 6641999872 | bytes 1 | tf_op jit(solution)/shard_map/partial/pallas_call | solution.py:56
  88.4 4.3 %all-to-all-start.2 = ((bf16[8,56,2048]{2,1,0:T(8,128)(2,1)}), bf16[8,56,2048]{2,1,0:T(8,128)(2,1)}, u32[]{:S(2)}, u32[]{:S(2)}) async-start(bf16[8,56,2048]{2,1,0:T(8,128)(2,1)} %bitcast.24), calls=%async_computation.2 | async-start | bytes 3670016 | tf_op jit(solution)/shard_map/all_to_all | solution.py:241
  100.9 6.1 %collective-permute-done.9.more = bf16[3,112,768]{2,1,0:T(8,128)(2,1)S(1)} collective-permute-done((bf16[3,112,768]{2,1,0:T(8,128)(2,1)}, bf16[3,112,768]{2,1,0:T(8,128)(2,1)S(1)}, u32[]{:S(2)}, u32[]{:S(2)}) %collective-permute-start.9) | collective-permute-done | bytes 516128 | tf_op jit(solution)/shard_map/ppermute | solution.py:237
  113.1 4.1 %all-to-all-done.2 = bf16[8,56,2048]{2,1,0:T(8,128)(2,1)} async-done(((bf16[8,56,2048]{2,1,0:T(8,128)(2,1)}), bf16[8,56,2048]{2,1,0:T(8,128)(2,1)}, u32[]{:S(2)}, u32[]{:S(2)}) %all-to-all-start.2) | async-done | bytes 1835040 | tf_op jit(solution)/shard_map/all_to_all | solution.py:241
  117.2 8.8 %collective-permute-done.10.near.refs_1_ = bf16[3,112,768]{2,1,0:T(8,128)(2,1)} collective-permute-done((bf16[3,112,768]{2,1,0:T(8,128)(2,1)}, bf16[3,112,768]{2,1,0:T(8,128)(2,1)}, u32[]{:S(2)}, u32[]{:S(2)}) %collective-permute-start.10) | collective-permute-done | bytes 516128 | tf_op jit(solution)/shard_map/ppermute | solution.py:237
  126.0 6.3 %partial.5 = (bf16[3,224,768]{2,1,0:T(8,128)(2,1)}, bf16[3,224,768]{2,1,0:T(8,128)(2,1)}) custom-call(s32[2]{0:T(128)S(1)} %pad_add_fusion.side, bf16[448,2048]{1,0:T(8,128)(2,1)} %bitcast.10.rows_ref.refs_14_, bf16[1,1024,768]{2,1,0:T(8,128)(2,1)S(1)} %copy-done.1, bf16[1,1024,768]{2,1,0:T(8,128)(2,1)S(1)} %copy-done.3, bf16[1,768,1024]{2,1,0:T(8,128)(2,1)} %down.5), custom_call_target="tpu_custom_call" | custom-call | flops 6641999872 | bytes 1 | tf_op jit(solution)/shard_map/partial/pallas_call | solution.py:56
  135.3 5.5 %input_grad.3 = bf16[448,1024]{1,0:T(8,128)(2,1)} custom-call(s32[2]{0:T(128)S(1)} %pad_add_fusion.side, bf16[3,112,768]{2,1,0:T(8,128)(2,1)S(1)} %copy-done.9, bf16[3,112,768]{2,1,0:T(8,128)(2,1)} %collective-permute-done.10.near.refs_1_, bf16[3,112,768]{2,1,0:T(8,128)(2,1)} %collective-permute-done.11.far.refs_2_, ...), custom_call_target="tpu_custom_call" | custom-call | flops 66419998720 | bytes 1 | tf_op jit(solution)/shard_map/input_grad/pallas_call | solution.py:56
  142.4 4.9 %collective-permute-done.14.got = bf16[3,224,768]{2,1,0:T(8,128)(2,1)S(1)} collective-permute-done((bf16[3,224,768]{2,1,0:T(8,128)(2,1)}, bf16[3,224,768]{2,1,0:T(8,128)(2,1)S(1)}, u32[]{:S(2)}, u32[]{:S(2)}) %collective-permute-start.14) | collective-permute-done | bytes 1032224 | tf_op jit(solution)/shard_map/ppermute | solution.py:237
  152.8 4.7 %all-to-all-start.3 = ((bf16[8,56,1024]{2,1,0:T(8,128)(2,1)}), bf16[8,56,1024]{2,1,0:T(8,128)(2,1)S(1)}, u32[]{:S(2)}, u32[]{:S(2)}) async-start(bf16[8,56,1024]{2,1,0:T(8,128)(2,1)} %bitcast.27), calls=%async_computation.3 | async-start | bytes 1835008 | tf_op jit(solution)/shard_map/all_to_all | solution.py:241
  157.5 8.4 %collective-permute-done.16.near.refs_5_ = bf16[3,80,768]{2,1,0:T(8,128)(2,1)} collective-permute-done((bf16[3,80,768]{2,1,0:T(8,128)(2,1)}, bf16[3,80,768]{2,1,0:T(8,128)(2,1)}, u32[]{:S(2)}, u32[]{:S(2)}) %collective-permute-start.16) | collective-permute-done | bytes 368672 | tf_op jit(solution)/shard_map/ppermute | solution.py:237
  183.4 5.3 %input_grad.4 = bf16[320,1024]{1,0:T(8,128)(2,1)} custom-call(s32[2]{0:T(128)S(1)} %pad_add_fusion.side, bf16[3,80,768]{2,1,0:T(8,128)(2,1)} %back.4.own.refs_4_, bf16[3,80,768]{2,1,0:T(8,128)(2,1)} %collective-permute-done.16.near.refs_5_, bf16[3,80,768]{2,1,0:T(8,128)(2,1)} %collective-permute-done.17.far.refs_6_, ...), custom_call_target="tpu_custom_call" | custom-call | flops 66419998720 | bytes 1 | tf_op jit(solution)/shard_map/input_grad/pallas_call | solution.py:56
  188.7 5.5 %all-to-all-start.4 = ((bf16[8,40,1024]{2,1,0:T(8,128)(2,1)}), bf16[8,40,1024]{2,1,0:T(8,128)(2,1)S(1)}, u32[]{:S(2)}, u32[]{:S(2)}) async-start(bf16[8,40,1024]{2,1,0:T(8,128)(2,1)} %bitcast.29), calls=%async_computation.4 | async-start | bytes 1310720 | tf_op jit(solution)/shard_map/all_to_all | solution.py:241
  194.2 5.5 %input_grad.5 = bf16[448,1024]{1,0:T(8,128)(2,1)} custom-call(s32[2]{0:T(128)S(1)} %pad_add_fusion.side, bf16[3,112,768]{2,1,0:T(8,128)(2,1)S(1)} %copy-done.13, bf16[3,112,768]{2,1,0:T(8,128)(2,1)} %collective-permute-done.19.near.refs_9_, bf16[3,112,768]{2,1,0:T(8,128)(2,1)S(1)} %collective-permute-done.20.far.refs_10_, ...), custom_call_target="tpu_custom_call" | custom-call | flops 66419998720 | bytes 1 | tf_op jit(solution)/shard_map/input_grad/pallas_call | solution.py:56
  199.7 6.2 %all-to-all-done.4 = bf16[8,40,1024]{2,1,0:T(8,128)(2,1)S(1)} async-done(((bf16[8,40,1024]{2,1,0:T(8,128)(2,1)}), bf16[8,40,1024]{2,1,0:T(8,128)(2,1)S(1)}, u32[]{:S(2)}, u32[]{:S(2)}) %all-to-all-start.4) | async-done | bytes 655392 | tf_op jit(solution)/shard_map/all_to_all | solution.py:241
  214.9 9.1 %all-to-all-done.5 = bf16[8,56,1024]{2,1,0:T(8,128)(2,1)S(1)} async-done(((bf16[8,56,1024]{2,1,0:T(8,128)(2,1)}), bf16[8,56,1024]{2,1,0:T(8,128)(2,1)S(1)}, u32[]{:S(2)}, u32[]{:S(2)}) %all-to-all-start.5) | async-done | bytes 917536 | tf_op jit(solution)/shard_map/all_to_all | solution.py:241
  225.3 6.1 %collective-permute-start.26 = (bf16[128,1024]{1,0:T(8,128)(2,1)}, bf16[128,1024]{1,0:T(8,128)(2,1)S(1)}, u32[]{:S(2)}, u32[]{:S(2)}) collective-permute-start(bf16[128,1024]{1,0:T(8,128)(2,1)} %get-tuple-element.89), channel_id=1, source_target_pairs={{0,160},{1,161},{2,162},{3,163},{4,164},{5,165},{6,166},{7,167},{8... | collective-permute-start | bytes 786440 | tf_op jit(solution)/shard_map/ppermute | solution.py:230
  234.7 12.2 %fisher.1 = (bf16[1,1024,768]{2,1,0:T(8,128)(2,1)}, bf16[1,1024,768]{2,1,0:T(8,128)(2,1)}, bf16[1,768,1024]{2,1,0:T(8,128)(2,1)}) custom-call(s32[2]{0:T(128)S(1)} %pad_add_fusion.side, bf16[3,112,768]{2,1,0:T(8,128)(2,1)S(1)} %copy-done.10, bf16[3,112,768]{2,1,0:T(8,128)(2,1)} %collective-permute-done.10.near.refs_1_, ...), custom_call_target="tpu_custom_call" | custom-call | flops 123984003072 | bytes 1 | tf_op jit(solution)/shard_map/fisher/pallas_call | solution.py:56
  246.8 17.3 %collective-permute-done.27.refs_6_ = bf16[128,1024]{1,0:T(8,128)(2,1)S(1)} collective-permute-done((bf16[128,1024]{1,0:T(8,128)(2,1)}, bf16[128,1024]{1,0:T(8,128)(2,1)S(1)}, u32[]{:S(2)}, u32[]{:S(2)}) %collective-permute-start.27) | collective-permute-done | bytes 262176 | tf_op jit(solution)/shard_map/ppermute | solution.py:230
  (129 shorter events, 91.6 us)
Async XLA Ops:
  19.5 17.3 %collective-permute-start.4 = (bf16[272,1024]{1,0:T(8,128)(2,1)S(1)}, bf16[272,1024]{1,0:T(8,128)(2,1)S(1)}, u32[]{:S(2)}, u32[]{:S(2)}) collective-permute-start(bf16[272,1024]{1,0:T(8,128)(2,1)S(1)} %collective-permute-done.1.refs_2_), channel_id=1, source_target_pairs={{0,224},{1,225},{2,226},{3,227},{4,228},{5,229},{6,230},{7,231},{8... | collective-permute-start | bytes 1671176 | tf_op jit(solution)/shard_map/ppermute | solution.py:230
  26.3 29.0 %all-to-all-start.1 = ((bf16[8,56,2048]{2,1,0:T(8,128)(2,1)}), bf16[8,56,2048]{2,1,0:T(8,128)(2,1)}, u32[]{:S(2)}, u32[]{:S(2)}) async-start(bf16[8,56,2048]{2,1,0:T(8,128)(2,1)} %bitcast.25), calls=%async_computation.1 | async-start | bytes 3670016 | tf_op jit(solution)/shard_map/all_to_all | solution.py:241
  35.3 24.5 %collective-permute-start.3 = (bf16[272,1024]{1,0:T(8,128)(2,1)}, bf16[272,1024]{1,0:T(8,128)(2,1)}, u32[]{:S(2)}, u32[]{:S(2)}) collective-permute-start(bf16[272,1024]{1,0:T(8,128)(2,1)} %collective-permute-done.2.refs_0_), channel_id=1, source_target_pairs={{0,32},{1,33},{2,34},{3,35},{4,36},{5,37},{6,38},{7,39},{8,40},{9,... | collective-permute-start | bytes 1671176 | tf_op jit(solution)/shard_map/ppermute | solution.py:230
  55.2 22.3 %all-to-all-start = ((bf16[8,40,2048]{2,1,0:T(8,128)(2,1)}), bf16[8,40,2048]{2,1,0:T(8,128)(2,1)S(1)}, u32[]{:S(2)}, u32[]{:S(2)}) async-start(bf16[8,40,2048]{2,1,0:T(8,128)(2,1)} %bitcast.26), calls=%async_computation | async-start | bytes 2621440 | tf_op jit(solution)/shard_map/all_to_all | solution.py:241
  58.9 25.6 %collective-permute-start.5 = (bf16[272,1024]{1,0:T(8,128)(2,1)S(1)}, bf16[272,1024]{1,0:T(8,128)(2,1)}, u32[]{:S(2)}, u32[]{:S(2)}) collective-permute-start(bf16[272,1024]{1,0:T(8,128)(2,1)S(1)} %collective-permute-done.4.refs_1_), channel_id=1, source_target_pairs={{0,224},{1,225},{2,226},{3,227},{4,228},{5,229},{6,230},{7,231},{8... | collective-permute-start | bytes 1671176 | tf_op jit(solution)/shard_map/ppermute | solution.py:230
  59.7 24.8 %collective-permute-start.6 = (bf16[272,1024]{1,0:T(8,128)(2,1)}, bf16[272,1024]{1,0:T(8,128)(2,1)}, u32[]{:S(2)}, u32[]{:S(2)}) collective-permute-start(bf16[272,1024]{1,0:T(8,128)(2,1)} %collective-permute-done.3.refs_0_), channel_id=1, source_target_pairs={{0,32},{1,33},{2,34},{3,35},{4,36},{5,37},{6,38},{7,39},{8,40},{9,... | collective-permute-start | bytes 1671176 | tf_op jit(solution)/shard_map/ppermute | solution.py:230
  70.0 22.7 %collective-permute-start.7 = (bf16[3,224,768]{2,1,0:T(8,128)(2,1)}, bf16[3,224,768]{2,1,0:T(8,128)(2,1)}, u32[]{:S(2)}, u32[]{:S(2)}) collective-permute-start(bf16[3,224,768]{2,1,0:T(8,128)(2,1)} %get-tuple-element.61), channel_id=1, source_target_pairs={{0,1},{1,0},{2,3},{3,2},{4,7},{5,6},{6,5},{7,4},{8,9},{9,8},{10,11... | collective-permute-start | bytes 3096584 | tf_op jit(solution)/shard_map/ppermute | solution.py:237
  88.4 28.7 %all-to-all-start.2 = ((bf16[8,56,2048]{2,1,0:T(8,128)(2,1)}), bf16[8,56,2048]{2,1,0:T(8,128)(2,1)}, u32[]{:S(2)}, u32[]{:S(2)}) async-start(bf16[8,56,2048]{2,1,0:T(8,128)(2,1)} %bitcast.24), calls=%async_computation.2 | async-start | bytes 3670016 | tf_op jit(solution)/shard_map/all_to_all | solution.py:241
  112.0 28.8 %collective-permute-start.13 = (bf16[3,80,768]{2,1,0:T(8,128)(2,1)}, bf16[3,80,768]{2,1,0:T(8,128)(2,1)S(1)}, u32[]{:S(2)}, u32[]{:S(2)}) collective-permute-start(bf16[3,80,768]{2,1,0:T(8,128)(2,1)} %pair.4), channel_id=1, source_target_pairs={{0,3},{1,2},{2,1},{3,0},{4,5},{5,4},{6,7},{7,6},{8,11},{9,10},{10,... | collective-permute-start | bytes 1105928 | tf_op jit(solution)/shard_map/ppermute | solution.py:237
  113.1 21.3 %collective-permute-start.11 = (bf16[3,112,768]{2,1,0:T(8,128)(2,1)}, bf16[3,112,768]{2,1,0:T(8,128)(2,1)}, u32[]{:S(2)}, u32[]{:S(2)}) collective-permute-start(bf16[3,112,768]{2,1,0:T(8,128)(2,1)} %back.3.own.refs_0_), channel_id=1, source_target_pairs={{0,1},{1,0},{2,3},{3,2},{4,7},{5,6},{6,5},{7,4},{8,9},{9,8},{10,11... | collective-permute-start | bytes 1548296 | tf_op jit(solution)/shard_map/ppermute | solution.py:237
  148.7 17.2 %collective-permute-start.15 = (bf16[3,112,768]{2,1,0:T(8,128)(2,1)}, bf16[3,112,768]{2,1,0:T(8,128)(2,1)S(1)}, u32[]{:S(2)}, u32[]{:S(2)}) collective-permute-start(bf16[3,112,768]{2,1,0:T(8,128)(2,1)} %pair.5), channel_id=1, source_target_pairs={{0,3},{1,2},{2,1},{3,0},{4,5},{5,4},{6,7},{7,6},{8,11},{9,10},{10,... | collective-permute-start | bytes 1548296 | tf_op jit(solution)/shard_map/ppermute | solution.py:237
  152.0 25.0 %collective-permute-start.17 = (bf16[3,80,768]{2,1,0:T(8,128)(2,1)}, bf16[3,80,768]{2,1,0:T(8,128)(2,1)}, u32[]{:S(2)}, u32[]{:S(2)}) collective-permute-start(bf16[3,80,768]{2,1,0:T(8,128)(2,1)} %back.4.own.refs_4_), channel_id=1, source_target_pairs={{0,1},{1,0},{2,3},{3,2},{4,7},{5,6},{6,5},{7,4},{8,9},{9,8},{10,11... | collective-permute-start | bytes 1105928 | tf_op jit(solution)/shard_map/ppermute | solution.py:237
  152.8 21.2 %all-to-all-start.3 = ((bf16[8,56,1024]{2,1,0:T(8,128)(2,1)}), bf16[8,56,1024]{2,1,0:T(8,128)(2,1)S(1)}, u32[]{:S(2)}, u32[]{:S(2)}) async-start(bf16[8,56,1024]{2,1,0:T(8,128)(2,1)} %bitcast.27), calls=%async_computation.3 | async-start | bytes 1835008 | tf_op jit(solution)/shard_map/all_to_all | solution.py:241
  165.9 17.5 %collective-permute-start.18 = (bf16[3,80,768]{2,1,0:T(8,128)(2,1)}, bf16[3,80,768]{2,1,0:T(8,128)(2,1)}, u32[]{:S(2)}, u32[]{:S(2)}) collective-permute-start(bf16[3,80,768]{2,1,0:T(8,128)(2,1)} %collective-permute-done.16.near.refs_5_), channel_id=1, source_target_pairs={{0,1},{1,0},{2,3},{3,2},{4,7},{5,6},{6,5},{7,4},{8,9},{9,8},{10,11... | collective-permute-start | bytes 1105928 | tf_op jit(solution)/shard_map/ppermute | solution.py:237
  170.0 24.2 %collective-permute-start.20 = (bf16[3,112,768]{2,1,0:T(8,128)(2,1)}, bf16[3,112,768]{2,1,0:T(8,128)(2,1)S(1)}, u32[]{:S(2)}, u32[]{:S(2)}) collective-permute-start(bf16[3,112,768]{2,1,0:T(8,128)(2,1)} %back.5.own.refs_8_), channel_id=1, source_target_pairs={{0,1},{1,0},{2,3},{3,2},{4,7},{5,6},{6,5},{7,4},{8,9},{9,8},{10,11... | collective-permute-start | bytes 1548296 | tf_op jit(solution)/shard_map/ppermute | solution.py:237
  176.2 55.2 %collective-permute-start.22 = (bf16[128,1024]{1,0:T(8,128)(2,1)}, bf16[128,1024]{1,0:T(8,128)(2,1)}, u32[]{:S(2)}, u32[]{:S(2)}) collective-permute-start(bf16[128,1024]{1,0:T(8,128)(2,1)} %get-tuple-element.93), channel_id=1, source_target_pairs={{0,224},{1,225},{2,226},{3,227},{4,228},{5,229},{6,230},{7,231},{8... | collective-permute-start | bytes 786440 | tf_op jit(solution)/shard_map/ppermute | solution.py:230
  177.0 54.4 %collective-permute-start.23 = (bf16[128,1024]{1,0:T(8,128)(2,1)}, bf16[128,1024]{1,0:T(8,128)(2,1)}, u32[]{:S(2)}, u32[]{:S(2)}) collective-permute-start(bf16[128,1024]{1,0:T(8,128)(2,1)} %get-tuple-element.94), channel_id=1, source_target_pairs={{0,32},{1,33},{2,34},{3,35},{4,36},{5,37},{6,38},{7,39},{8,40},{9,... | collective-permute-start | bytes 786440 | tf_op jit(solution)/shard_map/ppermute | solution.py:230
  188.7 17.2 %all-to-all-start.4 = ((bf16[8,40,1024]{2,1,0:T(8,128)(2,1)}), bf16[8,40,1024]{2,1,0:T(8,128)(2,1)S(1)}, u32[]{:S(2)}, u32[]{:S(2)}) async-start(bf16[8,40,1024]{2,1,0:T(8,128)(2,1)} %bitcast.29), calls=%async_computation.4 | async-start | bytes 1310720 | tf_op jit(solution)/shard_map/all_to_all | solution.py:241
  206.0 18.0 %all-to-all-start.5 = ((bf16[8,56,1024]{2,1,0:T(8,128)(2,1)}), bf16[8,56,1024]{2,1,0:T(8,128)(2,1)S(1)}, u32[]{:S(2)}, u32[]{:S(2)}) async-start(bf16[8,56,1024]{2,1,0:T(8,128)(2,1)} %bitcast.28), calls=%async_computation.5 | async-start | bytes 1835008 | tf_op jit(solution)/shard_map/all_to_all | solution.py:241
  210.7 36.1 %collective-permute-start.24 = (bf16[128,1024]{1,0:T(8,128)(2,1)}, bf16[128,1024]{1,0:T(8,128)(2,1)S(1)}, u32[]{:S(2)}, u32[]{:S(2)}) collective-permute-start(bf16[128,1024]{1,0:T(8,128)(2,1)} %get-tuple-element.87), channel_id=1, source_target_pairs={{0,192},{1,193},{2,194},{3,195},{4,196},{5,197},{6,198},{7,199},{8... | collective-permute-start | bytes 786440 | tf_op jit(solution)/shard_map/ppermute | solution.py:230
  214.1 32.8 %collective-permute-start.25 = (bf16[128,1024]{1,0:T(8,128)(2,1)}, bf16[128,1024]{1,0:T(8,128)(2,1)S(1)}, u32[]{:S(2)}, u32[]{:S(2)}) collective-permute-start(bf16[128,1024]{1,0:T(8,128)(2,1)} %get-tuple-element.95), channel_id=1, source_target_pairs={{0,64},{1,65},{2,66},{3,67},{4,68},{5,69},{6,70},{7,71},{8,72},{9,... | collective-permute-start | bytes 786440 | tf_op jit(solution)/shard_map/ppermute | solution.py:230
  225.3 38.9 %collective-permute-start.26 = (bf16[128,1024]{1,0:T(8,128)(2,1)}, bf16[128,1024]{1,0:T(8,128)(2,1)S(1)}, u32[]{:S(2)}, u32[]{:S(2)}) collective-permute-start(bf16[128,1024]{1,0:T(8,128)(2,1)} %get-tuple-element.89), channel_id=1, source_target_pairs={{0,160},{1,161},{2,162},{3,163},{4,164},{5,165},{6,166},{7,167},{8... | collective-permute-start | bytes 786440 | tf_op jit(solution)/shard_map/ppermute | solution.py:230
  231.4 32.8 %collective-permute-start.27 = (bf16[128,1024]{1,0:T(8,128)(2,1)}, bf16[128,1024]{1,0:T(8,128)(2,1)S(1)}, u32[]{:S(2)}, u32[]{:S(2)}) collective-permute-start(bf16[128,1024]{1,0:T(8,128)(2,1)} %get-tuple-element.96), channel_id=1, source_target_pairs={{0,96},{1,97},{2,98},{3,99},{4,100},{5,101},{6,102},{7,103},{8,104... | collective-permute-start | bytes 786440 | tf_op jit(solution)/shard_map/ppermute | solution.py:230
  231.4 32.8 %collective-permute-start.28 = (bf16[128,1024]{1,0:T(8,128)(2,1)}, bf16[128,1024]{1,0:T(8,128)(2,1)S(1)}, u32[]{:S(2)}, u32[]{:S(2)}) collective-permute-start(bf16[128,1024]{1,0:T(8,128)(2,1)} %get-tuple-element.97), channel_id=1, source_target_pairs={{0,128},{1,129},{2,130},{3,131},{4,132},{5,133},{6,134},{7,135},{8... | collective-permute-start | bytes 786440 | tf_op jit(solution)/shard_map/ppermute | solution.py:230
  (41 other events, 377.0 us)

commit v4 on v3

--- a/solution.py
+++ b/solution.py
@@ -38,7 +38,6 @@
     ('combine', 1),
     ('combine', 2),
     ('fisher', 0),
-    ('total', False),
     ('total', True),
 )
 

time: 270 us -> 268 us (level)
    unnamed x60 -> x58, local copies, waits for them, and re-layouts: 12.3 us -> 11.3 us
    pallas_call x22 -> x21, Pallas kernels: 74.8 us -> 74 us  [call(): pl.pallas_call(body, out_shape=[pltpu.HBM(o.shape, o.dtype) for o in outs...]
where the time goes in v4:
time: 268 us; the launch traced here: 266 us
  waiting for transfers between devices  109 us (41%)
  Pallas kernels  74 us (28%)
  starting transfers between devices  71.4 us (27%)
  local copies, waits for them, and re-layouts  11.3 us (4%)
    pallas_call x21, Pallas kernels, call(): pl.pallas_call(body, out_shape=[pltpu.HBM(o.shape, o.dtype) for o in outs...  74 us
    all_to_all x6, waiting for transfers between devices, across(): lax.all_to_all(split, 'ep', split_axis=0, concat_axis=0, axis_index_group...  41 us
    ppermute x14, waiting for transfers between devices, along_z(): lax.ppermute(value, ('ep', 'tp'), [(i, (i + step * GROUP * tp) % n) for i...  34.6 us
    ppermute x15, waiting for transfers between devices, along_x(): return lax.ppermute(value, ('ep', 'tp'), pairs)  33 us
    ppermute x14, starting transfers between devices, along_z(): lax.ppermute(value, ('ep', 'tp'), [(i, (i + step * GROUP * tp) % n) for i...  26.8 us
    all_to_all x6, starting transfers between devices, across(): lax.all_to_all(split, 'ep', split_axis=0, concat_axis=0, axis_index_group...  26.1 us
    ppermute x15, starting transfers between devices, along_x(): return lax.ppermute(value, ('ep', 'tp'), pairs)  18.4 us
    unnamed x58, local copies, waits for them, and re-layouts  11.3 us
  transfers between devices with their start and end apart: 35, of which 14 were waited for; matrix products, arithmetic and copies ran while one was open for 0% of the time, Pallas kernels for 26%

profile of v4, /device:TPU:64, one launch (start us, length us, event | category | flops | bytes accessed | tf_op | source)
XLA Modules:
  0.0 266.2 jit_solution(6463093389745924771)
XLA Ops:
  6.8 12.7 %collective-permute-done.1.refs_2_ = bf16[272,1024]{1,0:T(8,128)(2,1)S(1)} collective-permute-done((bf16[272,1024]{1,0:T(8,128)(2,1)}, bf16[272,1024]{1,0:T(8,128)(2,1)S(1)}, u32[]{:S(2)}, u32[]{:S(2)}) %collective-permute-start.1) | collective-permute-done | bytes 557088 | tf_op jit(solution)/shard_map/ppermute | solution.py:229
  26.3 4.5 %all-to-all-start.1 = ((bf16[8,56,2048]{2,1,0:T(8,128)(2,1)}), bf16[8,56,2048]{2,1,0:T(8,128)(2,1)}, u32[]{:S(2)}, u32[]{:S(2)}) async-start(bf16[8,56,2048]{2,1,0:T(8,128)(2,1)} %bitcast.25), calls=%async_computation.1 | async-start | bytes 3670016 | tf_op jit(solution)/shard_map/all_to_all | solution.py:240
  30.7 4.5 %collective-permute-done.2.refs_0_ = bf16[272,1024]{1,0:T(8,128)(2,1)} collective-permute-done((bf16[272,1024]{1,0:T(8,128)(2,1)S(1)}, bf16[272,1024]{1,0:T(8,128)(2,1)}, u32[]{:S(2)}, u32[]{:S(2)}) %collective-permute-start.2) | collective-permute-done | bytes 557088 | tf_op jit(solution)/shard_map/ppermute | solution.py:229
  39.6 15.7 %all-to-all-done.1 = bf16[8,56,2048]{2,1,0:T(8,128)(2,1)} async-done(((bf16[8,56,2048]{2,1,0:T(8,128)(2,1)}), bf16[8,56,2048]{2,1,0:T(8,128)(2,1)}, u32[]{:S(2)}, u32[]{:S(2)}) %all-to-all-start.1) | async-done | bytes 1835040 | tf_op jit(solution)/shard_map/all_to_all | solution.py:240
  63.7 6.3 %partial.3 = (bf16[3,224,768]{2,1,0:T(8,128)(2,1)}, bf16[3,224,768]{2,1,0:T(8,128)(2,1)}) custom-call(s32[2]{0:T(128)S(1)} %pad_add_fusion.side, bf16[448,2048]{1,0:T(8,128)(2,1)} %bitcast.8.rows_ref.refs_12_, bf16[1,1024,768]{2,1,0:T(8,128)(2,1)S(1)} %copy-done.1, bf16[1,1024,768]{2,1,0:T(8,128)(2,1)S(1)} %copy-done.2, bf16[1,768,1024]{2,1,0:T(8,128)(2,1)} %down.5), custom_call_target="tpu_custom_call" | custom-call | flops 6641999872 | bytes 1 | tf_op jit(solution)/shard_map/partial/pallas_call | solution.py:55
  71.5 6.0 %all-to-all-done = bf16[8,40,2048]{2,1,0:T(8,128)(2,1)S(1)} async-done(((bf16[8,40,2048]{2,1,0:T(8,128)(2,1)}), bf16[8,40,2048]{2,1,0:T(8,128)(2,1)S(1)}, u32[]{:S(2)}, u32[]{:S(2)}) %all-to-all-start) | async-done | bytes 1310752 | tf_op jit(solution)/shard_map/all_to_all | solution.py:240
  77.5 5.5 %partial.4 = (bf16[3,160,768]{2,1,0:T(8,128)(2,1)}, bf16[3,160,768]{2,1,0:T(8,128)(2,1)}) custom-call(s32[2]{0:T(128)S(1)} %pad_add_fusion.side, bf16[320,2048]{1,0:T(8,128)(2,1)S(1)} %bitcast.17, bf16[1,1024,768]{2,1,0:T(8,128)(2,1)S(1)} %copy-done.1, bf16[1,1024,768]{2,1,0:T(8,128)(2,1)} %up.11, bf16[1,768,1024]{2,1,0:T(8,128)(2,1)} %down.5), custom_call_target="tpu_custom_call" | custom-call | flops 6641999872 | bytes 1 | tf_op jit(solution)/shard_map/partial/pallas_call | solution.py:55
  88.4 4.3 %all-to-all-start.2 = ((bf16[8,56,2048]{2,1,0:T(8,128)(2,1)}), bf16[8,56,2048]{2,1,0:T(8,128)(2,1)}, u32[]{:S(2)}, u32[]{:S(2)}) async-start(bf16[8,56,2048]{2,1,0:T(8,128)(2,1)} %bitcast.24), calls=%async_computation.2 | async-start | bytes 3670016 | tf_op jit(solution)/shard_map/all_to_all | solution.py:240
  100.9 6.2 %collective-permute-done.9.more = bf16[3,112,768]{2,1,0:T(8,128)(2,1)S(1)} collective-permute-done((bf16[3,112,768]{2,1,0:T(8,128)(2,1)}, bf16[3,112,768]{2,1,0:T(8,128)(2,1)S(1)}, u32[]{:S(2)}, u32[]{:S(2)}) %collective-permute-start.9) | collective-permute-done | bytes 516128 | tf_op jit(solution)/shard_map/ppermute | solution.py:236
  113.1 4.0 %all-to-all-done.2 = bf16[8,56,2048]{2,1,0:T(8,128)(2,1)} async-done(((bf16[8,56,2048]{2,1,0:T(8,128)(2,1)}), bf16[8,56,2048]{2,1,0:T(8,128)(2,1)}, u32[]{:S(2)}, u32[]{:S(2)}) %all-to-all-start.2) | async-done | bytes 1835040 | tf_op jit(solution)/shard_map/all_to_all | solution.py:240
  117.2 8.8 %collective-permute-done.10.near.refs_1_ = bf16[3,112,768]{2,1,0:T(8,128)(2,1)} collective-permute-done((bf16[3,112,768]{2,1,0:T(8,128)(2,1)}, bf16[3,112,768]{2,1,0:T(8,128)(2,1)}, u32[]{:S(2)}, u32[]{:S(2)}) %collective-permute-start.10) | collective-permute-done | bytes 516128 | tf_op jit(solution)/shard_map/ppermute | solution.py:236
  126.0 6.3 %partial.5 = (bf16[3,224,768]{2,1,0:T(8,128)(2,1)}, bf16[3,224,768]{2,1,0:T(8,128)(2,1)}) custom-call(s32[2]{0:T(128)S(1)} %pad_add_fusion.side, bf16[448,2048]{1,0:T(8,128)(2,1)} %bitcast.10.rows_ref.refs_14_, bf16[1,1024,768]{2,1,0:T(8,128)(2,1)S(1)} %copy-done.1, bf16[1,1024,768]{2,1,0:T(8,128)(2,1)S(1)} %copy-done.3, bf16[1,768,1024]{2,1,0:T(8,128)(2,1)} %down.5), custom_call_target="tpu_custom_call" | custom-call | flops 6641999872 | bytes 1 | tf_op jit(solution)/shard_map/partial/pallas_call | solution.py:55
  135.3 5.5 %input_grad.3 = bf16[448,1024]{1,0:T(8,128)(2,1)} custom-call(s32[2]{0:T(128)S(1)} %pad_add_fusion.side, bf16[3,112,768]{2,1,0:T(8,128)(2,1)S(1)} %copy-done.9, bf16[3,112,768]{2,1,0:T(8,128)(2,1)} %collective-permute-done.10.near.refs_1_, bf16[3,112,768]{2,1,0:T(8,128)(2,1)} %collective-permute-done.11.far.refs_2_, ...), custom_call_target="tpu_custom_call" | custom-call | flops 66419998720 | bytes 1 | tf_op jit(solution)/shard_map/input_grad/pallas_call | solution.py:55
  142.4 4.9 %collective-permute-done.14.got = bf16[3,224,768]{2,1,0:T(8,128)(2,1)S(1)} collective-permute-done((bf16[3,224,768]{2,1,0:T(8,128)(2,1)}, bf16[3,224,768]{2,1,0:T(8,128)(2,1)S(1)}, u32[]{:S(2)}, u32[]{:S(2)}) %collective-permute-start.14) | collective-permute-done | bytes 1032224 | tf_op jit(solution)/shard_map/ppermute | solution.py:236
  152.8 4.7 %all-to-all-start.3 = ((bf16[8,56,1024]{2,1,0:T(8,128)(2,1)}), bf16[8,56,1024]{2,1,0:T(8,128)(2,1)S(1)}, u32[]{:S(2)}, u32[]{:S(2)}) async-start(bf16[8,56,1024]{2,1,0:T(8,128)(2,1)} %bitcast.27), calls=%async_computation.3 | async-start | bytes 1835008 | tf_op jit(solution)/shard_map/all_to_all | solution.py:240
  157.5 8.4 %collective-permute-done.16.near.refs_5_ = bf16[3,80,768]{2,1,0:T(8,128)(2,1)} collective-permute-done((bf16[3,80,768]{2,1,0:T(8,128)(2,1)}, bf16[3,80,768]{2,1,0:T(8,128)(2,1)}, u32[]{:S(2)}, u32[]{:S(2)}) %collective-permute-start.16) | collective-permute-done | bytes 368672 | tf_op jit(solution)/shard_map/ppermute | solution.py:236
  183.4 5.3 %input_grad.4 = bf16[320,1024]{1,0:T(8,128)(2,1)} custom-call(s32[2]{0:T(128)S(1)} %pad_add_fusion.side, bf16[3,80,768]{2,1,0:T(8,128)(2,1)} %back.4.own.refs_4_, bf16[3,80,768]{2,1,0:T(8,128)(2,1)} %collective-permute-done.16.near.refs_5_, bf16[3,80,768]{2,1,0:T(8,128)(2,1)} %collective-permute-done.17.far.refs_6_, ...), custom_call_target="tpu_custom_call" | custom-call | flops 66419998720 | bytes 1 | tf_op jit(solution)/shard_map/input_grad/pallas_call | solution.py:55
  188.7 5.5 %all-to-all-start.4 = ((bf16[8,40,1024]{2,1,0:T(8,128)(2,1)}), bf16[8,40,1024]{2,1,0:T(8,128)(2,1)S(1)}, u32[]{:S(2)}, u32[]{:S(2)}) async-start(bf16[8,40,1024]{2,1,0:T(8,128)(2,1)} %bitcast.29), calls=%async_computation.4 | async-start | bytes 1310720 | tf_op jit(solution)/shard_map/all_to_all | solution.py:240
  194.2 5.5 %input_grad.5 = bf16[448,1024]{1,0:T(8,128)(2,1)} custom-call(s32[2]{0:T(128)S(1)} %pad_add_fusion.side, bf16[3,112,768]{2,1,0:T(8,128)(2,1)S(1)} %copy-done.13, bf16[3,112,768]{2,1,0:T(8,128)(2,1)} %collective-permute-done.19.near.refs_9_, bf16[3,112,768]{2,1,0:T(8,128)(2,1)S(1)} %collective-permute-done.20.far.refs_10_, ...), custom_call_target="tpu_custom_call" | custom-call | flops 66419998720 | bytes 1 | tf_op jit(solution)/shard_map/input_grad/pallas_call | solution.py:55
  199.7 6.2 %all-to-all-done.4 = bf16[8,40,1024]{2,1,0:T(8,128)(2,1)S(1)} async-done(((bf16[8,40,1024]{2,1,0:T(8,128)(2,1)}), bf16[8,40,1024]{2,1,0:T(8,128)(2,1)S(1)}, u32[]{:S(2)}, u32[]{:S(2)}) %all-to-all-start.4) | async-done | bytes 655392 | tf_op jit(solution)/shard_map/all_to_all | solution.py:240
  214.9 9.1 %all-to-all-done.5 = bf16[8,56,1024]{2,1,0:T(8,128)(2,1)S(1)} async-done(((bf16[8,56,1024]{2,1,0:T(8,128)(2,1)}), bf16[8,56,1024]{2,1,0:T(8,128)(2,1)S(1)}, u32[]{:S(2)}, u32[]{:S(2)}) %all-to-all-start.5) | async-done | bytes 917536 | tf_op jit(solution)/shard_map/all_to_all | solution.py:240
  225.3 6.1 %collective-permute-start.26 = (bf16[128,1024]{1,0:T(8,128)(2,1)}, bf16[128,1024]{1,0:T(8,128)(2,1)S(1)}, u32[]{:S(2)}, u32[]{:S(2)}) collective-permute-start(bf16[128,1024]{1,0:T(8,128)(2,1)} %get-tuple-element.89), channel_id=1, source_target_pairs={{0,160},{1,161},{2,162},{3,163},{4,164},{5,165},{6,166},{7,167},{8... | collective-permute-start | bytes 786440 | tf_op jit(solution)/shard_map/ppermute | solution.py:229
  234.7 12.2 %fisher.1 = (bf16[1,1024,768]{2,1,0:T(8,128)(2,1)}, bf16[1,1024,768]{2,1,0:T(8,128)(2,1)}, bf16[1,768,1024]{2,1,0:T(8,128)(2,1)}) custom-call(s32[2]{0:T(128)S(1)} %pad_add_fusion.side, bf16[3,112,768]{2,1,0:T(8,128)(2,1)S(1)} %copy-done.10, bf16[3,112,768]{2,1,0:T(8,128)(2,1)} %collective-permute-done.10.near.refs_1_, ...), custom_call_target="tpu_custom_call" | custom-call | flops 123984003072 | bytes 1 | tf_op jit(solution)/shard_map/fisher/pallas_call | solution.py:55
  246.8 17.3 %collective-permute-done.27.refs_6_ = bf16[128,1024]{1,0:T(8,128)(2,1)S(1)} collective-permute-done((bf16[128,1024]{1,0:T(8,128)(2,1)}, bf16[128,1024]{1,0:T(8,128)(2,1)S(1)}, u32[]{:S(2)}, u32[]{:S(2)}) %collective-permute-start.27) | collective-permute-done | bytes 262176 | tf_op jit(solution)/shard_map/ppermute | solution.py:229
  (126 shorter events, 89.8 us)
Async XLA Ops:
  19.5 17.3 %collective-permute-start.4 = (bf16[272,1024]{1,0:T(8,128)(2,1)S(1)}, bf16[272,1024]{1,0:T(8,128)(2,1)S(1)}, u32[]{:S(2)}, u32[]{:S(2)}) collective-permute-start(bf16[272,1024]{1,0:T(8,128)(2,1)S(1)} %collective-permute-done.1.refs_2_), channel_id=1, source_target_pairs={{0,224},{1,225},{2,226},{3,227},{4,228},{5,229},{6,230},{7,231},{8... | collective-permute-start | bytes 1671176 | tf_op jit(solution)/shard_map/ppermute | solution.py:229
  26.3 29.0 %all-to-all-start.1 = ((bf16[8,56,2048]{2,1,0:T(8,128)(2,1)}), bf16[8,56,2048]{2,1,0:T(8,128)(2,1)}, u32[]{:S(2)}, u32[]{:S(2)}) async-start(bf16[8,56,2048]{2,1,0:T(8,128)(2,1)} %bitcast.25), calls=%async_computation.1 | async-start | bytes 3670016 | tf_op jit(solution)/shard_map/all_to_all | solution.py:240
  35.3 24.5 %collective-permute-start.3 = (bf16[272,1024]{1,0:T(8,128)(2,1)}, bf16[272,1024]{1,0:T(8,128)(2,1)}, u32[]{:S(2)}, u32[]{:S(2)}) collective-permute-start(bf16[272,1024]{1,0:T(8,128)(2,1)} %collective-permute-done.2.refs_0_), channel_id=1, source_target_pairs={{0,32},{1,33},{2,34},{3,35},{4,36},{5,37},{6,38},{7,39},{8,40},{9,... | collective-permute-start | bytes 1671176 | tf_op jit(solution)/shard_map/ppermute | solution.py:229
  55.2 22.3 %all-to-all-start = ((bf16[8,40,2048]{2,1,0:T(8,128)(2,1)}), bf16[8,40,2048]{2,1,0:T(8,128)(2,1)S(1)}, u32[]{:S(2)}, u32[]{:S(2)}) async-start(bf16[8,40,2048]{2,1,0:T(8,128)(2,1)} %bitcast.26), calls=%async_computation | async-start | bytes 2621440 | tf_op jit(solution)/shard_map/all_to_all | solution.py:240
  58.9 25.6 %collective-permute-start.5 = (bf16[272,1024]{1,0:T(8,128)(2,1)S(1)}, bf16[272,1024]{1,0:T(8,128)(2,1)}, u32[]{:S(2)}, u32[]{:S(2)}) collective-permute-start(bf16[272,1024]{1,0:T(8,128)(2,1)S(1)} %collective-permute-done.4.refs_1_), channel_id=1, source_target_pairs={{0,224},{1,225},{2,226},{3,227},{4,228},{5,229},{6,230},{7,231},{8... | collective-permute-start | bytes 1671176 | tf_op jit(solution)/shard_map/ppermute | solution.py:229
  59.7 24.8 %collective-permute-start.6 = (bf16[272,1024]{1,0:T(8,128)(2,1)}, bf16[272,1024]{1,0:T(8,128)(2,1)}, u32[]{:S(2)}, u32[]{:S(2)}) collective-permute-start(bf16[272,1024]{1,0:T(8,128)(2,1)} %collective-permute-done.3.refs_0_), channel_id=1, source_target_pairs={{0,32},{1,33},{2,34},{3,35},{4,36},{5,37},{6,38},{7,39},{8,40},{9,... | collective-permute-start | bytes 1671176 | tf_op jit(solution)/shard_map/ppermute | solution.py:229
  70.0 22.7 %collective-permute-start.7 = (bf16[3,224,768]{2,1,0:T(8,128)(2,1)}, bf16[3,224,768]{2,1,0:T(8,128)(2,1)}, u32[]{:S(2)}, u32[]{:S(2)}) collective-permute-start(bf16[3,224,768]{2,1,0:T(8,128)(2,1)} %get-tuple-element.61), channel_id=1, source_target_pairs={{0,1},{1,0},{2,3},{3,2},{4,7},{5,6},{6,5},{7,4},{8,9},{9,8},{10,11... | collective-permute-start | bytes 3096584 | tf_op jit(solution)/shard_map/ppermute | solution.py:236
  88.4 28.7 %all-to-all-start.2 = ((bf16[8,56,2048]{2,1,0:T(8,128)(2,1)}), bf16[8,56,2048]{2,1,0:T(8,128)(2,1)}, u32[]{:S(2)}, u32[]{:S(2)}) async-start(bf16[8,56,2048]{2,1,0:T(8,128)(2,1)} %bitcast.24), calls=%async_computation.2 | async-start | bytes 3670016 | tf_op jit(solution)/shard_map/all_to_all | solution.py:240
  112.0 28.8 %collective-permute-start.13 = (bf16[3,80,768]{2,1,0:T(8,128)(2,1)}, bf16[3,80,768]{2,1,0:T(8,128)(2,1)S(1)}, u32[]{:S(2)}, u32[]{:S(2)}) collective-permute-start(bf16[3,80,768]{2,1,0:T(8,128)(2,1)} %pair.4), channel_id=1, source_target_pairs={{0,3},{1,2},{2,1},{3,0},{4,5},{5,4},{6,7},{7,6},{8,11},{9,10},{10,... | collective-permute-start | bytes 1105928 | tf_op jit(solution)/shard_map/ppermute | solution.py:236
  113.1 21.3 %collective-permute-start.11 = (bf16[3,112,768]{2,1,0:T(8,128)(2,1)}, bf16[3,112,768]{2,1,0:T(8,128)(2,1)}, u32[]{:S(2)}, u32[]{:S(2)}) collective-permute-start(bf16[3,112,768]{2,1,0:T(8,128)(2,1)} %back.3.own.refs_0_), channel_id=1, source_target_pairs={{0,1},{1,0},{2,3},{3,2},{4,7},{5,6},{6,5},{7,4},{8,9},{9,8},{10,11... | collective-permute-start | bytes 1548296 | tf_op jit(solution)/shard_map/ppermute | solution.py:236
  148.7 17.2 %collective-permute-start.15 = (bf16[3,112,768]{2,1,0:T(8,128)(2,1)}, bf16[3,112,768]{2,1,0:T(8,128)(2,1)S(1)}, u32[]{:S(2)}, u32[]{:S(2)}) collective-permute-start(bf16[3,112,768]{2,1,0:T(8,128)(2,1)} %pair.5), channel_id=1, source_target_pairs={{0,3},{1,2},{2,1},{3,0},{4,5},{5,4},{6,7},{7,6},{8,11},{9,10},{10,... | collective-permute-start | bytes 1548296 | tf_op jit(solution)/shard_map/ppermute | solution.py:236
  152.0 25.0 %collective-permute-start.17 = (bf16[3,80,768]{2,1,0:T(8,128)(2,1)}, bf16[3,80,768]{2,1,0:T(8,128)(2,1)}, u32[]{:S(2)}, u32[]{:S(2)}) collective-permute-start(bf16[3,80,768]{2,1,0:T(8,128)(2,1)} %back.4.own.refs_4_), channel_id=1, source_target_pairs={{0,1},{1,0},{2,3},{3,2},{4,7},{5,6},{6,5},{7,4},{8,9},{9,8},{10,11... | collective-permute-start | bytes 1105928 | tf_op jit(solution)/shard_map/ppermute | solution.py:236
  152.8 21.2 %all-to-all-start.3 = ((bf16[8,56,1024]{2,1,0:T(8,128)(2,1)}), bf16[8,56,1024]{2,1,0:T(8,128)(2,1)S(1)}, u32[]{:S(2)}, u32[]{:S(2)}) async-start(bf16[8,56,1024]{2,1,0:T(8,128)(2,1)} %bitcast.27), calls=%async_computation.3 | async-start | bytes 1835008 | tf_op jit(solution)/shard_map/all_to_all | solution.py:240
  165.9 17.5 %collective-permute-start.18 = (bf16[3,80,768]{2,1,0:T(8,128)(2,1)}, bf16[3,80,768]{2,1,0:T(8,128)(2,1)}, u32[]{:S(2)}, u32[]{:S(2)}) collective-permute-start(bf16[3,80,768]{2,1,0:T(8,128)(2,1)} %collective-permute-done.16.near.refs_5_), channel_id=1, source_target_pairs={{0,1},{1,0},{2,3},{3,2},{4,7},{5,6},{6,5},{7,4},{8,9},{9,8},{10,11... | collective-permute-start | bytes 1105928 | tf_op jit(solution)/shard_map/ppermute | solution.py:236
  170.0 24.2 %collective-permute-start.20 = (bf16[3,112,768]{2,1,0:T(8,128)(2,1)}, bf16[3,112,768]{2,1,0:T(8,128)(2,1)S(1)}, u32[]{:S(2)}, u32[]{:S(2)}) collective-permute-start(bf16[3,112,768]{2,1,0:T(8,128)(2,1)} %back.5.own.refs_8_), channel_id=1, source_target_pairs={{0,1},{1,0},{2,3},{3,2},{4,7},{5,6},{6,5},{7,4},{8,9},{9,8},{10,11... | collective-permute-start | bytes 1548296 | tf_op jit(solution)/shard_map/ppermute | solution.py:236
  176.2 55.2 %collective-permute-start.22 = (bf16[128,1024]{1,0:T(8,128)(2,1)}, bf16[128,1024]{1,0:T(8,128)(2,1)}, u32[]{:S(2)}, u32[]{:S(2)}) collective-permute-start(bf16[128,1024]{1,0:T(8,128)(2,1)} %get-tuple-element.93), channel_id=1, source_target_pairs={{0,224},{1,225},{2,226},{3,227},{4,228},{5,229},{6,230},{7,231},{8... | collective-permute-start | bytes 786440 | tf_op jit(solution)/shard_map/ppermute | solution.py:229
  177.0 54.4 %collective-permute-start.23 = (bf16[128,1024]{1,0:T(8,128)(2,1)}, bf16[128,1024]{1,0:T(8,128)(2,1)}, u32[]{:S(2)}, u32[]{:S(2)}) collective-permute-start(bf16[128,1024]{1,0:T(8,128)(2,1)} %get-tuple-element.94), channel_id=1, source_target_pairs={{0,32},{1,33},{2,34},{3,35},{4,36},{5,37},{6,38},{7,39},{8,40},{9,... | collective-permute-start | bytes 786440 | tf_op jit(solution)/shard_map/ppermute | solution.py:229
  188.7 17.2 %all-to-all-start.4 = ((bf16[8,40,1024]{2,1,0:T(8,128)(2,1)}), bf16[8,40,1024]{2,1,0:T(8,128)(2,1)S(1)}, u32[]{:S(2)}, u32[]{:S(2)}) async-start(bf16[8,40,1024]{2,1,0:T(8,128)(2,1)} %bitcast.29), calls=%async_computation.4 | async-start | bytes 1310720 | tf_op jit(solution)/shard_map/all_to_all | solution.py:240
  206.0 18.0 %all-to-all-start.5 = ((bf16[8,56,1024]{2,1,0:T(8,128)(2,1)}), bf16[8,56,1024]{2,1,0:T(8,128)(2,1)S(1)}, u32[]{:S(2)}, u32[]{:S(2)}) async-start(bf16[8,56,1024]{2,1,0:T(8,128)(2,1)} %bitcast.28), calls=%async_computation.5 | async-start | bytes 1835008 | tf_op jit(solution)/shard_map/all_to_all | solution.py:240
  210.7 36.1 %collective-permute-start.24 = (bf16[128,1024]{1,0:T(8,128)(2,1)}, bf16[128,1024]{1,0:T(8,128)(2,1)S(1)}, u32[]{:S(2)}, u32[]{:S(2)}) collective-permute-start(bf16[128,1024]{1,0:T(8,128)(2,1)} %get-tuple-element.87), channel_id=1, source_target_pairs={{0,192},{1,193},{2,194},{3,195},{4,196},{5,197},{6,198},{7,199},{8... | collective-permute-start | bytes 786440 | tf_op jit(solution)/shard_map/ppermute | solution.py:229
  214.1 32.8 %collective-permute-start.25 = (bf16[128,1024]{1,0:T(8,128)(2,1)}, bf16[128,1024]{1,0:T(8,128)(2,1)S(1)}, u32[]{:S(2)}, u32[]{:S(2)}) collective-permute-start(bf16[128,1024]{1,0:T(8,128)(2,1)} %get-tuple-element.95), channel_id=1, source_target_pairs={{0,64},{1,65},{2,66},{3,67},{4,68},{5,69},{6,70},{7,71},{8,72},{9,... | collective-permute-start | bytes 786440 | tf_op jit(solution)/shard_map/ppermute | solution.py:229
  225.3 38.9 %collective-permute-start.26 = (bf16[128,1024]{1,0:T(8,128)(2,1)}, bf16[128,1024]{1,0:T(8,128)(2,1)S(1)}, u32[]{:S(2)}, u32[]{:S(2)}) collective-permute-start(bf16[128,1024]{1,0:T(8,128)(2,1)} %get-tuple-element.89), channel_id=1, source_target_pairs={{0,160},{1,161},{2,162},{3,163},{4,164},{5,165},{6,166},{7,167},{8... | collective-permute-start | bytes 786440 | tf_op jit(solution)/shard_map/ppermute | solution.py:229
  231.4 32.8 %collective-permute-start.27 = (bf16[128,1024]{1,0:T(8,128)(2,1)}, bf16[128,1024]{1,0:T(8,128)(2,1)S(1)}, u32[]{:S(2)}, u32[]{:S(2)}) collective-permute-start(bf16[128,1024]{1,0:T(8,128)(2,1)} %get-tuple-element.96), channel_id=1, source_target_pairs={{0,96},{1,97},{2,98},{3,99},{4,100},{5,101},{6,102},{7,103},{8,104... | collective-permute-start | bytes 786440 | tf_op jit(solution)/shard_map/ppermute | solution.py:229
  231.4 32.8 %collective-permute-start.28 = (bf16[128,1024]{1,0:T(8,128)(2,1)}, bf16[128,1024]{1,0:T(8,128)(2,1)S(1)}, u32[]{:S(2)}, u32[]{:S(2)}) collective-permute-start(bf16[128,1024]{1,0:T(8,128)(2,1)} %get-tuple-element.97), channel_id=1, source_target_pairs={{0,128},{1,129},{2,130},{3,131},{4,132},{5,133},{6,134},{7,135},{8... | collective-permute-start | bytes 786440 | tf_op jit(solution)/shard_map/ppermute | solution.py:229
  (40 other events, 376.0 us)
